TPU v7x, 32 devices: a whole 2x2x4 slice. The times are simulated.
32 devices in a mesh: lvl: 4 (over z), gx: 4 (over y, core), gy: 2 (over x).
Axes of the slice: x: 2, y: 2, z: 4, core: 2. Of those that a mesh axis runs over, the one named last changes fastest.
Arguments:
- initial: float32 [256, 256, 256], P('gx', 'gy'), may hold values from -6 to 6
- reaction: float32 [256, 256, 256], P('gx', 'gy'), may hold values from -0.5 to 0
Outputs:
- levels: float32 [4, 256, 256, 256], P('lvl', 'gx', 'gy')
All inputs are finite; a program needn't handle non-finite values.
Results may differ from a plain program's by a relative error of at most 0.0001.
Values sent between devices are 32-bit elements; how exact they have to be, the bound alone decides.
No kernel may reach another device: no remote copies, remote signals or barrier semaphores. Data moves between devices by JAX's collectives and lax.ppermute only.
A program may use at most 64 MiB of HBM per device.

v0:
```python
import math

import jax
import jax.numpy as jnp
from jax import lax
from jax.sharding import PartitionSpec as P

STEPS = 1


DIFFUSE = 0.3
HIGHEST = lax.Precision.HIGHEST


def phases_at(points, length, count, first):
    wavenum = lax.broadcasted_iota(jnp.int32, (points.shape[0], count), 1) + first
    turns = points[:, None] * wavenum % length
    angles = turns.astype(jnp.float32) * (2.0 * math.pi / length)
    return (jnp.cos(angles), jnp.sin(angles))


def phases(length, count, first):
    points = lax.broadcasted_iota(jnp.int32, (length,), 0)
    return phases_at(points, length, count, first)


def table_from(cosine, sine, direction):
    turned = direction * sine
    return jnp.stack([jnp.stack([cosine, turned], axis=1), jnp.stack([-turned, cosine], axis=1)])


def spectral_factor(first_x, count_x, first_y, count_y, first_z, count_z, scales, norm):
    wave_z = (lax.broadcasted_iota(jnp.int32, (count_z, 1, 1), 0) + first_z).astype(
        jnp.float32
    ) / scales[2]
    wave_x = (lax.broadcasted_iota(jnp.int32, (1, count_x, 1), 1) + first_x).astype(
        jnp.float32
    ) / scales[0]
    wave_y = (lax.broadcasted_iota(jnp.int32, (1, 1, count_y), 2) + first_y).astype(
        jnp.float32
    ) / scales[1]
    factor_real = -DIFFUSE * (wave_x * wave_x + wave_y * wave_y + wave_z * wave_z) * norm
    factor_imag = -(0.3 * wave_x + 0.2 * wave_y + 0.25 * wave_z) * norm
    return (factor_real, factor_imag)


def shards(initial, reaction):
    rows_x, rows_y, depth = initial.shape
    parts_x = lax.axis_size("gx")
    parts_y = lax.axis_size("gy")
    level_count = lax.axis_size("lvl")
    full_x = rows_x * parts_x
    full_y = rows_y * parts_y
    modes_x = full_x // 2
    modes_y = full_y // 2
    modes_z = depth // 4
    scales = (full_x // 4, full_y // 4, depth // 4)
    norm = 1.0 / (full_x * full_y * depth)
    cosine_z, sine_z = phases(depth, modes_z, 0)
    forward_table = jnp.stack([cosine_z, -sine_z], axis=2)
    weights = jnp.where(lax.broadcasted_iota(jnp.int32, (1, modes_z), 1) == 0, 1.0, 2.0).astype(
        jnp.float32
    )
    back_z = jnp.stack([(cosine_z * weights).T, -(sine_z * weights).T], axis=1)
    cosine_y, sine_y = phases(full_y, modes_y, -(modes_y // 2))
    forward_y = table_from(cosine_y, sine_y, -1.0)
    back_y = table_from(cosine_y.T, sine_y.T, 1.0)
    block_x = modes_x // parts_y
    level_index = lax.axis_index("lvl")

    def make_rate(points, parts, joint_index, react):
        block_z = modes_z // parts
        cosine_x, sine_x = phases_at(points, full_x, modes_x, -(modes_x // 2))
        forward_x = table_from(cosine_x, sine_x, -1.0)
        back_x = table_from(cosine_x.T, sine_x.T, 1.0)
        z_back = back_z.reshape(parts, block_z, 2, depth)
        factor_real, factor_imag = spectral_factor(
            lax.axis_index("gy") * block_x - modes_x // 2,
            block_x,
            -(modes_y // 2),
            modes_y,
            joint_index * block_z,
            block_z,
            scales,
            norm,
        )

        def x_lines(block_data):
            return jnp.einsum("abpyx,pxqk->abqky", block_data, forward_x, precision=HIGHEST)

        def z_lines(block_data):
            return jnp.einsum("abpyx,abpz->xyz", block_data, z_back, precision=HIGHEST)

        def rate(grid_field):
            spectrum = jnp.einsum("xyz,zkp->kpyx", grid_field, forward_table, precision=HIGHEST)
            spectrum = spectrum.reshape(parts, block_z, 2, grid_field.shape[1], grid_field.shape[0])
            wide_form = x_lines(
                lax.all_to_all(spectrum, ("lvl", "gx"), split_axis=0, concat_axis=4, tiled=True)
            )
            tall_form = lax.all_to_all(wide_form, "gy", split_axis=3, concat_axis=4, tiled=True)
            tall_form = jnp.einsum("abpxy,pyqk->abqxk", tall_form, forward_y, precision=HIGHEST)
            real_part = tall_form[:, :, 0]
            imag_part = tall_form[:, :, 1]
            tall_form = jnp.stack(
                [
                    factor_real * real_part - factor_imag * imag_part,
                    factor_real * imag_part + factor_imag * real_part,
                ],
                axis=2,
            )
            tall_form = jnp.einsum("abpxk,pkqy->abqxy", tall_form, back_y, precision=HIGHEST)
            wide_form = lax.all_to_all(tall_form, "gy", split_axis=4, concat_axis=3, tiled=True)
            wide_form = jnp.einsum("abpky,pkqx->abqyx", wide_form, back_x, precision=HIGHEST)
            values = z_lines(
                lax.all_to_all(wide_form, ("lvl", "gx"), split_axis=4, concat_axis=0, tiled=True)
            )
            return values + react * grid_field

        return rate

    slab_rows = rows_x // level_count
    joint_parts = parts_x * level_count
    places = lax.broadcasted_iota(jnp.int32, (full_x,), 0)
    source = places // slab_rows
    points = source % parts_x * rows_x + source // parts_x * slab_rows + places % slab_rows
    joint_index = level_index * parts_x + lax.axis_index("gx")
    start = level_index * slab_rows
    own_initial = lax.dynamic_slice_in_dim(initial, start, slab_rows, 0)
    own_reaction = lax.dynamic_slice_in_dim(reaction, start, slab_rows, 0)
    slab_rate = make_rate(points, joint_parts, joint_index, own_reaction)
    start_rate = slab_rate(own_initial)
    earlier = None
    finals = []
    for level_number in range(level_count):
        current = own_initial
        rates = [start_rate]
        update = current + rates[0]
        if earlier is not None:
            update = update + 0.5 * (earlier[1] - earlier[0])
        current = update
        if level_number < level_count - 1 or 0 < STEPS - 1:
            rates.append(slab_rate(current))
        finals.append(current)
        earlier = rates
    stacked = jnp.stack(finals)
    return lax.all_to_all(stacked, "lvl", split_axis=0, concat_axis=1, tiled=True)


def solution(mesh):
    in_specs = (P("gx", "gy", None), P("gx", "gy", None))
    out_specs = P("lvl", "gx", "gy", None)
    return jax.shard_map(shards, mesh=mesh, in_specs=in_specs, out_specs=out_specs, check_vma=False)
```

profile of v0, /device:TPU:0, one launch (start us, length us, event | category | flops | bytes accessed | tf_op | source)
XLA Modules:
  0.0 650.5 jit_solution(11271549821165849705)
XLA Ops:
  0.3 3.9 fusion.16
  4.2 1.6 copy.127
  5.8 7.4 %all-to-all-start = ((f32[16,4,2,128,16]{3,4,2,1,0:T(8,128)}), f32[16,4,2,128,16]{3,4,2,1,0:T(8,128)S(1)}, u32[]{:S(2)}, u32[]{:S(2)}) async-start(f32[16,4,2,128,16]{3,4,2,1,0:T(8,128)} %copy.127), calls=%async_computation | async-start | bytes 2097152 | tf_op jit(solution)/shard_map/all_to_all | solution.py:98
  15.7 20.4 %all-to-all-done = f32[16,4,2,128,16]{3,4,2,1,0:T(8,128)S(1)} async-done(((f32[16,4,2,128,16]{3,4,2,1,0:T(8,128)}), f32[16,4,2,128,16]{3,4,2,1,0:T(8,128)S(1)}, u32[]{:S(2)}, u32[]{:S(2)}) %all-to-all-start) | async-done | bytes 1048608 | tf_op jit(solution)/shard_map/all_to_all | solution.py:98
  38.4 3.5 all-to-all-start.1
  42.0 9.0 %all-to-all-done.1 = f32[1,4,2,128,128]{4,1,2,0,3:T(4,128)S(1)} async-done(((f32[1,4,2,128,128]{4,1,2,0,3:T(4,128)}), f32[1,4,2,128,128]{4,1,2,0,3:T(4,128)S(1)}, u32[]{:S(2)}, u32[]{:S(2)}) %all-to-all-start.1) | async-done | bytes 524320 | tf_op jit(solution)/shard_map/all_to_all | solution.py:100
  53.7 1.7 reshape.1108
  55.5 3.7 all-to-all-start.2
  59.2 8.2 %all-to-all-done.2 = f32[2,1,65536]{2,1,0:T(1,128)S(1)} async-done(((f32[2,1,65536]{2,1,0:T(1,128)}), f32[2,1,65536]{2,1,0:T(1,128)S(1)}, u32[]{:S(2)}, u32[]{:S(2)}) %all-to-all-start.2) | async-done | bytes 524320 | tf_op jit(solution)/shard_map/all_to_all | solution.py:112
  67.9 2.2 reduce
  72.5 1.6 copy.137
  74.2 6.2 all-to-all-start.3
  80.7 22.6 %all-to-all-done.3 = f32[1,4,2,128,256]{3,1,2,0,4:T(4,128)S(1)} async-done(((f32[1,4,2,128,256]{3,1,2,0,4:T(4,128)}), f32[1,4,2,128,256]{3,1,2,0,4:T(4,128)S(1)}, u32[]{:S(2)}, u32[]{:S(2)}) %all-to-all-start.3) | async-done | bytes 1048608 | tf_op jit(solution)/shard_map/all_to_all | solution.py:115
  104.2 4.6 bitcast_add_fusion.3
  108.9 3.8 fusion.14
  113.3 31.4 %all_to_all.264 = f32[16,4,2,128,16]{3,4,2,1,0:T(8,128)S(1)} all-to-all(f32[16,4,2,128,16]{3,4,2,1,0:T(8,128)S(1)} %copy.141), channel_id=1, replica_groups=mesh['lvl'=4,'gx'=4,'gy'=2] {'lvl','gx'}, dimensions={0} | all-to-all | bytes 2097152 | tf_op jit(solution)/shard_map/all_to_all | solution.py:98
  146.2 12.2 %all_to_all.265 = f32[1,4,2,128,128]{4,1,2,0,3:T(4,128)S(1)} all-to-all(f32[1,4,2,128,128]{4,1,2,0,3:T(4,128)S(1)} %copy.144), channel_id=1, replica_groups=mesh['lvl'=4,'gx'=4,'gy'=2] {'gy'}, dimensions={3} | all-to-all | bytes 1048576 | tf_op jit(solution)/shard_map/all_to_all | solution.py:100
  159.6 2.3 reshape.1072
  161.9 1.7 convolution_bitcast_fusion.14
  164.4 1.4 convolution_bitcast_fusion.8
  165.9 2.4 copy.148
  168.2 2.7 reshape.1110
  170.9 12.8 %all_to_all.266 = f32[2,1,65536]{2,1,0:T(1,128)} all-to-all(f32[2,1,65536]{2,1,0:T(1,128)} %reshape.1110), channel_id=1, replica_groups=mesh['lvl'=4,'gx'=4,'gy'=2] {'gy'}, dimensions={0} | all-to-all | bytes 1048576 | tf_op jit(solution)/shard_map/all_to_all | solution.py:112
  183.8 3.9 reduce.1
  187.7 2.9 reshape.1111
  190.6 2.3 copy.149
  192.9 2.2 convolution_bitcast_fusion.2
  195.8 28.5 %all_to_all.267 = f32[1,4,2,128,256]{3,1,2,0,4:T(4,128)S(1)} all-to-all(f32[1,4,2,128,256]{3,1,2,0,4:T(4,128)S(1)} %copy.151), channel_id=1, replica_groups=mesh['lvl'=4,'gx'=4,'gy'=2] {'lvl','gx'}, dimensions={4} | all-to-all | bytes 2097152 | tf_op jit(solution)/shard_map/all_to_all | solution.py:115
  224.4 4.7 fusion.9
  229.1 2.2 fusion.12
  232.0 29.6 %all_to_all.268 = f32[16,4,2,128,16]{3,4,2,1,0:T(8,128)S(1)} all-to-all(f32[16,4,2,128,16]{3,4,2,1,0:T(8,128)S(1)} %copy.155), channel_id=1, replica_groups=mesh['lvl'=4,'gx'=4,'gy'=2] {'lvl','gx'}, dimensions={0} | all-to-all | bytes 2097152 | tf_op jit(solution)/shard_map/all_to_all | solution.py:98
  263.1 11.8 %all_to_all.269 = f32[1,4,2,128,128]{4,1,2,0,3:T(4,128)S(1)} all-to-all(f32[1,4,2,128,128]{4,1,2,0,3:T(4,128)S(1)} %copy.158), channel_id=1, replica_groups=mesh['lvl'=4,'gx'=4,'gy'=2] {'gy'}, dimensions={3} | all-to-all | bytes 1048576 | tf_op jit(solution)/shard_map/all_to_all | solution.py:100
  276.1 2.3 reshape.1084
  278.4 1.7 convolution_bitcast_fusion.13
  280.9 1.4 convolution_bitcast_fusion.6
  282.4 2.4 copy.162
  284.7 2.7 reshape.1112
  287.4 13.0 %all_to_all.270 = f32[2,1,65536]{2,1,0:T(1,128)} all-to-all(f32[2,1,65536]{2,1,0:T(1,128)} %reshape.1112), channel_id=1, replica_groups=mesh['lvl'=4,'gx'=4,'gy'=2] {'gy'}, dimensions={0} | all-to-all | bytes 1048576 | tf_op jit(solution)/shard_map/all_to_all | solution.py:112
  300.4 3.9 reduce.2
  304.4 2.9 reshape.1113
  307.2 2.3 copy.163
  309.6 2.2 convolution_bitcast_fusion.1
  312.5 28.4 %all_to_all.271 = f32[1,4,2,128,256]{3,1,2,0,4:T(4,128)S(1)} all-to-all(f32[1,4,2,128,256]{3,1,2,0,4:T(4,128)S(1)} %copy.165), channel_id=1, replica_groups=mesh['lvl'=4,'gx'=4,'gy'=2] {'lvl','gx'}, dimensions={4} | all-to-all | bytes 2097152 | tf_op jit(solution)/shard_map/all_to_all | solution.py:115
  340.9 4.8 fusion.6
  345.7 2.2 fusion.10
  348.6 29.6 %all_to_all.272 = f32[16,4,2,128,16]{3,4,2,1,0:T(8,128)S(1)} all-to-all(f32[16,4,2,128,16]{3,4,2,1,0:T(8,128)S(1)} %copy.169), channel_id=1, replica_groups=mesh['lvl'=4,'gx'=4,'gy'=2] {'lvl','gx'}, dimensions={0} | all-to-all | bytes 2097152 | tf_op jit(solution)/shard_map/all_to_all | solution.py:98
  379.7 12.0 %all_to_all.273 = f32[1,4,2,128,128]{4,1,2,0,3:T(4,128)S(1)} all-to-all(f32[1,4,2,128,128]{4,1,2,0,3:T(4,128)S(1)} %copy.172), channel_id=1, replica_groups=mesh['lvl'=4,'gx'=4,'gy'=2] {'gy'}, dimensions={3} | all-to-all | bytes 1048576 | tf_op jit(solution)/shard_map/all_to_all | solution.py:100
  391.8 1.2 copy.303
  393.0 2.3 reshape.1096
  395.2 1.7 convolution_bitcast_fusion.12
  397.8 1.4 convolution_bitcast_fusion.4
  399.2 1.5 copy.176
  400.8 1.7 reshape.1114
  402.5 12.8 %all_to_all.274 = f32[2,1,65536]{2,1,0:T(1,128)} all-to-all(f32[2,1,65536]{2,1,0:T(1,128)} %reshape.1114), channel_id=1, replica_groups=mesh['lvl'=4,'gx'=4,'gy'=2] {'gy'}, dimensions={0} | all-to-all | bytes 1048576 | tf_op jit(solution)/shard_map/all_to_all | solution.py:112
  415.3 3.2 reduce.3
  418.5 1.9 reshape.1115
  420.4 1.5 copy.177
  423.0 1.7 copy.179
  424.7 3.9 all-to-all-start.15
  428.6 3.2 fusion.76
  431.8 19.7 %all-to-all-done.15 = f32[1,4,2,128,256]{3,1,2,0,4:T(4,128)S(1)} async-done(((f32[1,4,2,128,256]{3,1,2,0,4:T(4,128)}), f32[1,4,2,128,256]{3,1,2,0,4:T(4,128)S(1)}, u32[]{:S(2)}, u32[]{:S(2)}) %all-to-all-start.15) | async-done | bytes 1048608 | tf_op jit(solution)/shard_map/all_to_all | solution.py:115
  451.4 5.3 fusion.3
  457.8 188.9 %all_to_all.275 = f32[4,16,128,256]{3,2,1,0:T(8,128)S(1)} all-to-all(f32[4,16,128,256]{3,2,1,0:T(8,128)S(1)} %pad_maximum_fusion), channel_id=1, replica_groups=mesh['lvl'=4,'gx'=4,'gy'=2] {'lvl'}, dimensions={0} | all-to-all | bytes 16777216 | tf_op jit(solution)/shard_map/all_to_all | solution.py:146
  646.6 3.4 copy.308
  (101 shorter events, 26.7 us)
Async XLA Ops:
  0.3 5.5 copy-start.15
  0.3 5.5 copy-start.19
  5.8 30.3 %all-to-all-start = ((f32[16,4,2,128,16]{3,4,2,1,0:T(8,128)}), f32[16,4,2,128,16]{3,4,2,1,0:T(8,128)S(1)}, u32[]{:S(2)}, u32[]{:S(2)}) async-start(f32[16,4,2,128,16]{3,4,2,1,0:T(8,128)} %copy.127), calls=%async_computation | async-start | bytes 2097152 | tf_op jit(solution)/shard_map/all_to_all | solution.py:98
  15.6 21.6 %copy-start.6 = (f32[1,256,2,128]{1,3,0,2:T(8,128)}, f32[1,256,2,128]{1,3,0,2:T(8,128)S(1)}, u32[]{:S(2)}) copy-start(f32[1,256,2,128]{1,3,0,2:T(8,128)S(1)} %get-tuple-element.20) | copy-start | bytes 786436
  15.7 36.7 %copy-start.23 = (f32[64,128]{1,0:T(8,128)}, f32[64,128]{1,0:T(8,128)S(1)}, u32[]{:S(2)}) copy-start(f32[64,128]{1,0:T(8,128)S(1)} %broadcast_add_fusion.1) | copy-start | bytes 98308
  38.4 12.6 %all-to-all-start.1 = ((f32[1,4,2,128,128]{4,1,2,0,3:T(4,128)}), f32[1,4,2,128,128]{4,1,2,0,3:T(4,128)S(1)}, u32[]{:S(2)}, u32[]{:S(2)}) async-start(f32[1,4,2,128,128]{4,1,2,0,3:T(4,128)} %copy.130), calls=%async_computation.1 | async-start | bytes 1048576 | tf_op jit(solution)/shard_map/all_to_all | solution.py:100
  42.0 10.6 %copy-start.24 = (f32[64,128]{1,0:T(8,128)}, f32[64,128]{1,0:T(8,128)S(1)}, u32[]{:S(2)}) copy-start(f32[64,128]{1,0:T(8,128)S(1)} %broadcast_add_fusion) | copy-start | bytes 98308
  55.5 11.9 %all-to-all-start.2 = ((f32[2,1,65536]{2,1,0:T(1,128)}), f32[2,1,65536]{2,1,0:T(1,128)S(1)}, u32[]{:S(2)}, u32[]{:S(2)}) async-start(f32[2,1,65536]{2,1,0:T(1,128)} %reshape.1108), calls=%async_computation.2 | async-start | bytes 1048576 | tf_op jit(solution)/shard_map/all_to_all | solution.py:112
  59.2 12.3 %copy-start.10 = (f32[1,128,2,256]{3,1,2,0:T(8,128)}, f32[1,128,2,256]{3,1,2,0:T(8,128)S(1)}, u32[]{:S(2)}) copy-start(f32[1,128,2,256]{3,1,2,0:T(8,128)S(1)} %get-tuple-element.13) | copy-start | bytes 786436
  59.2 12.3 %copy-start.12 = (f32[1,128,2,256]{3,1,2,0:T(8,128)}, f32[1,128,2,256]{3,1,2,0:T(8,128)S(1)}, u32[]{:S(2)}) copy-start(f32[1,128,2,256]{3,1,2,0:T(8,128)S(1)} %get-tuple-element.14) | copy-start | bytes 786436
  74.2 29.1 %all-to-all-start.3 = ((f32[1,4,2,128,256]{3,1,2,0,4:T(4,128)}), f32[1,4,2,128,256]{3,1,2,0,4:T(4,128)S(1)}, u32[]{:S(2)}, u32[]{:S(2)}) async-start(f32[1,4,2,128,256]{3,1,2,0,4:T(4,128)} %copy.137), calls=%async_computation.3 | async-start | bytes 2097152 | tf_op jit(solution)/shard_map/all_to_all | solution.py:115
  103.3 1.0 copy-start.14
  104.2 4.6 copy-start.16
  104.2 4.7 copy-start.20
  113.3 31.5 %copy-start.7 = (f32[1,256,2,128]{1,3,0,2:T(8,128)S(1)}, f32[1,256,2,128]{1,3,0,2:T(8,128)}, u32[]{:S(2)}) copy-start(f32[1,256,2,128]{1,3,0,2:T(8,128)} %copy-done.6) | copy-start | bytes 786436
  224.4 4.7 copy-start.17
  224.4 4.7 copy-start.21
  229.1 2.9 copy-start
  232.0 29.7 %copy-start.8 = (f32[1,256,2,128]{1,3,0,2:T(8,128)S(1)}, f32[1,256,2,128]{1,3,0,2:T(8,128)}, u32[]{:S(2)}) copy-start(f32[1,256,2,128]{1,3,0,2:T(8,128)} %copy-done.6) | copy-start | bytes 786436
  311.8 29.1 %copy-start.1 = (f32[16,128,256]{2,1,0:T(8,128)S(1)}, f32[16,128,256]{2,1,0:T(8,128)}, u32[]{:S(2)}) copy-start(f32[16,128,256]{2,1,0:T(8,128)} %copy-done) | copy-start | bytes 6291460
  340.9 4.8 copy-start.18
  340.9 4.8 copy-start.22
  345.7 2.9 copy-start.3
  348.6 29.8 %copy-start.9 = (f32[1,256,2,128]{1,3,0,2:T(8,128)S(1)}, f32[1,256,2,128]{1,3,0,2:T(8,128)}, u32[]{:S(2)}) copy-start(f32[1,256,2,128]{1,3,0,2:T(8,128)} %copy-done.6) | copy-start | bytes 786436
  415.3 6.6 %copy-start.11 = (f32[1,128,2,256]{3,1,2,0:T(8,128)S(1)}, f32[1,128,2,256]{3,1,2,0:T(8,128)}, u32[]{:S(2)}) copy-start(f32[1,128,2,256]{3,1,2,0:T(8,128)} %copy-done.10) | copy-start | bytes 786436
  415.3 6.6 %copy-start.13 = (f32[1,128,2,256]{3,1,2,0:T(8,128)S(1)}, f32[1,128,2,256]{3,1,2,0:T(8,128)}, u32[]{:S(2)}) copy-start(f32[1,128,2,256]{3,1,2,0:T(8,128)} %copy-done.12) | copy-start | bytes 786436
  424.7 26.8 %all-to-all-start.15 = ((f32[1,4,2,128,256]{3,1,2,0,4:T(4,128)}), f32[1,4,2,128,256]{3,1,2,0,4:T(4,128)S(1)}, u32[]{:S(2)}, u32[]{:S(2)}) async-start(f32[1,4,2,128,256]{3,1,2,0,4:T(4,128)} %copy.179), calls=%async_computation.15 | async-start | bytes 2097152 | tf_op jit(solution)/shard_map/all_to_all | solution.py:115
  451.4 5.3 copy-start.2
  451.4 5.4 copy-start.4
  451.4 5.4 copy-start.5
where the time goes:
time: 660 us; the launch traced here: 650 us
  blocking collectives  411 us (62%)
  waiting for transfers between devices  79.8 us (12%)
  local copies, waits for them, and re-layouts  57.6 us (9%)
  matrix products  52.7 us (8%)
  starting transfers between devices  24.7 us (4%)
  other arithmetic  23.3 us (4%)
    all_to_all x1, blocking collectives, shards(): lax.all_to_all(stacked, 'lvl', split_axis=0, concat_axis=1, tiled=True)  189 us
    all_to_all x3, blocking collectives, rate(): lax.all_to_all(spectrum, ('lvl', 'gx'), split_axis=0, concat_axis=4, tile...  90.7 us
    all_to_all x2, blocking collectives, rate(): lax.all_to_all(wide_form, ('lvl', 'gx'), split_axis=4, concat_axis=0, til...  56.9 us
    all_to_all x2, waiting for transfers between devices, rate(): lax.all_to_all(wide_form, ('lvl', 'gx'), split_axis=4, concat_axis=0, til...  42.3 us
    all_to_all x3, blocking collectives, rate(): lax.all_to_all(tall_form, 'gy', split_axis=4, concat_axis=3, tiled=True)  38.6 us
    all_to_all x3, blocking collectives, rate(): lax.all_to_all(wide_form, 'gy', split_axis=3, concat_axis=4, tiled=True)  36 us
    unnamed x59, local copies, waits for them, and re-layouts  21.8 us
    all_to_all x1, waiting for transfers between devices, rate(): lax.all_to_all(spectrum, ('lvl', 'gx'), split_axis=0, concat_axis=4, tile...  20.4 us
  transfers between devices with their start and end apart: 5, of which 5 were waited for; matrix products, arithmetic and copies ran while one was open for 1% of the time, Pallas kernels for 0%

commit v1 on v0

v1 whole, which is shorter than its diff:
```python
import math

import jax
import jax.numpy as jnp
from jax import lax
from jax.sharding import PartitionSpec as P

DIFFUSE = 0.3
PRECISION = lax.Precision.HIGH


def cos_sin(points, waves, length):
    turns = points[:, None] * waves[None, :] % length
    angles = turns.astype(jnp.float32) * (2.0 * math.pi / length)
    return jnp.cos(angles), jnp.sin(angles)


def complex_table(cosine, sine, direction):
    turned = direction * sine
    return jnp.stack([jnp.stack([cosine, turned], axis=1), jnp.stack([-turned, cosine], axis=1)])


def contract(spec, left, right):
    return jnp.einsum(spec, left, right, precision=PRECISION)


def swap(block, axes, mask):
    count = lax.axis_size(axes)
    return lax.ppermute(block, axes, [(i, i ^ mask) for i in range(count)])


def iota(count):
    return lax.broadcasted_iota(jnp.int32, (count,), 0)


def shards(initial, reaction):
    rows_x, rows_y, depth = initial.shape
    parts_x = lax.axis_size("gx")
    parts_y = lax.axis_size("gy")
    levels = lax.axis_size("lvl")
    full_x, full_y = rows_x * parts_x, rows_y * parts_y
    modes_x, modes_y, modes_z = full_x // 2, full_y // 2, depth // 4
    norm = 1.0 / (full_x * full_y * depth)
    level, at_x, at_y = (lax.axis_index(a) for a in ("lvl", "gx", "gy"))

    pair = at_x & 1
    extra = [("gx", 1 << k) for k in range(2, parts_x.bit_length() - 1)]
    extra += [("gy", 1 << k) for k in range(1, parts_y.bit_length() - 1)]
    place = ((at_x >> 1) & 1) * 2 + (at_y & 1)
    for axis, mask in extra:
        place = place * 2 + (lax.axis_index(axis) // mask & 1)
    blocks = parts_x // 2 * parts_y
    block_x = modes_x // blocks
    block_z = modes_z // levels
    half_z = block_z // 2

    waves_x = iota(modes_x)
    waves_x = ((waves_x // block_x) ^ place) * block_x + waves_x % block_x - modes_x // 2
    waves_y = iota(modes_y) - modes_y // 2
    near = pair * half_z + iota(half_z)
    far = (1 - pair) * half_z + iota(half_z)
    points_x = jnp.concatenate([at_x * rows_x + iota(rows_x), (at_x ^ 1) * rows_x + iota(rows_x)])
    points_y = at_y * rows_y + iota(rows_y)

    cosine, sine = cos_sin(jnp.concatenate([near, far]) + level * block_z, iota(depth), depth)
    forward_z = jnp.stack([cosine, -sine], axis=1).reshape(2, half_z, 2, depth)
    cosine_y, sine_y = cos_sin(points_y, waves_y, full_y)
    forward_y = complex_table(cosine_y, sine_y, -1.0)
    cosine_x, sine_x = cos_sin(points_x, waves_x, full_x)
    forward_x = complex_table(cosine_x, sine_x, -1.0)
    back_x = complex_table(cosine_x.T, sine_x.T, 1.0)
    back_y = complex_table(cosine_y.T, sine_y.T, 1.0)
    lots = [(level ^ m) * block_z for m in range(levels)]
    waves_z = jnp.concatenate([lot + near for lot in lots] + [lot + far for lot in lots])
    cosine, sine = cos_sin(waves_z, iota(depth), depth)
    weights = jnp.where(waves_z == 0, 1.0, 2.0).astype(jnp.float32)[:, None]
    back_z = jnp.stack([cosine * weights, -sine * weights], axis=1)

    own_z = (level * block_z + near)[:, None, None]
    own_x = waves_x[:block_x][None, :, None]
    own_y = waves_y[None, None, :]
    unit_x = own_x.astype(jnp.float32) / (full_x // 4)
    unit_y = own_y.astype(jnp.float32) / (full_y // 4)
    unit_z = own_z.astype(jnp.float32) / (depth // 4)
    factor_real = -DIFFUSE * (unit_x * unit_x + unit_y * unit_y + unit_z * unit_z) * norm
    factor_imag = -(0.3 * unit_x + 0.2 * unit_y + 0.25 * unit_z) * norm
    edge = (own_z == 0) & ((own_x == -(modes_x // 2)) | (own_y == -(modes_y // 2)))
    again = jnp.where(edge, 0.5, 1.0).astype(jnp.float32)[:, None] / norm

    def forward(field):
        planes = contract("hkpz,xyz->hkpxy", forward_z, field)
        other = swap(planes[1], "gx", 1)
        planes = jnp.concatenate([planes[0], other], axis=2)
        planes = contract("kpxy,pyqm->kqxm", planes, forward_y)
        planes = contract("kpxm,pxqj->kqjm", planes, forward_x)
        quarter = modes_x // 4
        pieces = [planes[:, :, i * quarter : (i + 1) * quarter] for i in range(4)]
        total = pieces[0] + swap(pieces[1], "gy", 1) + swap(pieces[2], "gx", 2)
        total = total + swap(pieces[3], ("gx", "gy"), 2 * parts_y + 1)
        for axis, mask in extra:
            middle = total.shape[2] // 2
            total = total[:, :, :middle] + swap(total[:, :, middle:], axis, mask)
        return total

    def scaled(spectrum):
        real, imag = spectrum[:, 0], spectrum[:, 1]
        return jnp.stack(
            [
                factor_real * real - factor_imag * imag,
                factor_real * imag + factor_imag * real,
            ],
            axis=1,
        )

    def gather(piece):
        for axis, mask in reversed(extra):
            piece = jnp.concatenate([piece, swap(piece, axis, mask)], axis=2)
        found = []
        for m in range(levels):
            lot = piece if m == 0 else swap(piece, "lvl", m)
            by_y = swap(lot, "gy", 1)
            by_x = swap(lot, "gx", 2)
            cross = swap(by_y, "gx", 2) if m % 2 == 0 else swap(by_x, "gy", 1)
            found.append([lot, by_y, by_x, cross])
        return found

    def back(found):
        modes = jnp.concatenate([jnp.concatenate(lot, axis=2) for lot in found], axis=0)
        lines = contract("npjm,pjqx->nqxm", modes, back_x)
        lines = contract("npxm,pmqy->nqxy", lines, back_y)
        other = swap(lines[:, :, rows_x:], "gx", 1)
        lines = jnp.concatenate([lines[:, :, :rows_x], other], axis=0)
        return contract("npxy,npz->xyz", lines, back_z)

    first = scaled(forward(initial))
    first_found = gather(first)
    second = scaled(again * first + forward(reaction * initial))
    second_found = gather(second)
    rate = back(first_found) + reaction * initial
    third = scaled(again * second + forward(reaction * rate))
    third_found = gather(third)
    rate_again = back(second_found) + reaction * rate
    fourth = scaled(again * third + forward(reaction * rate_again))
    fourth_found = gather(fourth)
    total = initial + rate + jnp.where(level >= 1, 0.5, 0.0) * rate_again
    rate_third = back(third_found) + reaction * rate_again
    rate_fourth = back(fourth_found) + reaction * rate_third
    total = total + jnp.where(level >= 2, 0.25, 0.0) * rate_third
    total = total + jnp.where(level >= 3, 0.125, 0.0) * rate_fourth
    return total[None]


def solution(mesh):
    in_specs = (P("gx", "gy", None), P("gx", "gy", None))
    out_specs = P("lvl", "gx", "gy", None)
    return jax.shard_map(shards, mesh=mesh, in_specs=in_specs, out_specs=out_specs, check_vma=False)
```

time: 660 us -> 392 us (0.59); the launches traced: 650 us -> 389 us
  blocking collectives: 411 us -> 0 us
  waiting for transfers between devices: 79.8 us -> 163 us
  starting transfers between devices: 24.7 us -> 90.8 us
  matrix products: 52.7 us -> 111 us
  local copies, waits for them, and re-layouts: 57.6 us -> 8.38 us
  other arithmetic: 23.3 us -> 13.9 us
    all_to_all x12 -> x0, blocking collectives: 411 us -> none  [the longest x1 189 us: shards(): lax.all_to_all(stacked, 'lvl', split_axis=0, concat_axis=1, tiled=True)]
    ppermute x0 -> x80, waiting for transfers between devices: none -> 163 us  [swap(): return lax.ppermute(block, axes, [(i, i ^ mask) for i in range(count)])]
    ppermute x0 -> x80, starting transfers between devices: none -> 90.8 us  [swap(): return lax.ppermute(block, axes, [(i, i ^ mask) for i in range(count)])]
    all_to_all x5 -> x0, waiting for transfers between devices: 79.8 us -> none  [the longest x2 42.3 us: rate(): lax.all_to_all(wide_form, ('lvl', 'gx'), split_axis=4, concat_axis=0, til...]
    dot_general x24, matrix products: 52.7 us -> 111 us  [contract(): return jnp.einsum(spec, left, right, precision=PRECISION)]
    all_to_all x5 -> x0, starting transfers between devices: 24.7 us -> none  [the longest x2 10.1 us: rate(): lax.all_to_all(wide_form, ('lvl', 'gx'), split_axis=4, concat_axis=0, til...]
    unnamed x59 -> x50, local copies, waits for them, and re-layouts: 21.8 us -> 1.5 us
    transpose x12 -> x0, local copies, waits for them, and re-layouts: 13.6 us -> none  [the longest x4 6.76 us: rate(): jnp.einsum('abpxk,pkqy->abqxy', tall_form, back_y, precision=HIGHEST)]
  transfers between devices with their start and end apart: 5 -> 80, of which waited for: 5 -> 44; matrix products, arithmetic and copies ran while one was open for 1% -> 9% of each run, Pallas kernels for 0% -> 0%
where the time goes in v1:
time: 392 us; the launch traced here: 389 us
  waiting for transfers between devices  163 us (42%)
  matrix products  111 us (28%)
  starting transfers between devices  90.8 us (23%)
  other arithmetic  13.9 us (4%)
  local copies, waits for them, and re-layouts  8.38 us (2%)
    ppermute x80, waiting for transfers between devices, swap(): return lax.ppermute(block, axes, [(i, i ^ mask) for i in range(count)])  163 us
    dot_general x24, matrix products, contract(): return jnp.einsum(spec, left, right, precision=PRECISION)  111 us
    ppermute x80, starting transfers between devices, swap(): return lax.ppermute(block, axes, [(i, i ^ mask) for i in range(count)])  90.8 us
    concatenate x4, other arithmetic, back(): lines = jnp.concatenate([lines[:, :, :rows_x], other], axis=0)  9.31 us
  transfers between devices with their start and end apart: 80, of which 44 were waited for; matrix products, arithmetic and copies ran while one was open for 9% of the time, Pallas kernels for 0%

profile of v1, /device:TPU:0, one launch (start us, length us, event | category | flops | bytes accessed | tf_op | source)
XLA Modules:
  0.0 389.1 jit_solution(4586291904688170241)
XLA Ops:
  0.4 7.0 %fusion.6 = f32[2,8,2,64,128]{4,1,3,2,0:T(8,128)S(1)} fusion(f32[64,128,256]{2,1,0:T(8,128)} %param.2, f32[2,8,1,256]{3,1,2,0:T(8,128)S(1)} %get-tuple-element.72, f32[2,8,1,256]{3,1,2,0:T(8,128)S(1)} %get-tuple-element.71), kind=kOutput, calls=%fused_computation.6 | convolution fusion | flops 402661376 | bytes 9469952 | tf_op jit(solution)/shard_map/hkpz,xyz->hkpxy/dot_general | solution.py:24
  8.0 6.5 %fusion.4 = f32[2,8,2,64,128]{4,1,3,2,0:T(8,128)S(1)} fusion(f32[64,128,256]{2,1,0:T(8,128)} %param.3, f32[64,128,256]{2,1,0:T(8,128)S(1)} %copy-done, f32[2,8,1,256]{3,1,2,0:T(8,128)S(1)} %get-tuple-element.72, f32[2,8,1,256]{3,1,2,0:T(8,128)S(1)} %get-tuple-element.71), kind=kOutput, calls=%fused_computation.4 | convolution fusion | flops 404758528 | bytes 17858560 | tf_op jit(solution)/shard_map/hkpz,xyz->hkpxy/dot_general | solution.py:24
  18.9 3.0 collective-permute-start.1
  24.9 2.0 collective-permute-start.21
  29.1 3.0 collective-permute-start.23
  32.0 4.7 %collective-permute-done.2 = f32[8,2,32,128]{3,2,0,1:T(8,128)S(1)} collective-permute-done((f32[8,2,32,128]{3,2,0,1:T(8,128)S(1)}, f32[8,2,32,128]{3,2,0,1:T(8,128)S(1)}, u32[]{:S(2)}, u32[]{:S(2)}) %collective-permute-start.2) | collective-permute-done | bytes 262176 | tf_op jit(solution)/shard_map/ppermute | solution.py:29
  37.0 3.4 collective-permute-done.21
  40.4 6.4 %collective-permute-done.22 = f32[8,2,32,128]{3,2,0,1:T(8,128)S(1)} collective-permute-done((f32[8,2,32,128]{3,2,0,1:T(8,128)S(1)}, f32[8,2,32,128]{3,2,0,1:T(8,128)S(1)}, u32[]{:S(2)}, u32[]{:S(2)}) %collective-permute-start.22) | collective-permute-done | bytes 262176 | tf_op jit(solution)/shard_map/ppermute | solution.py:29
  48.5 2.6 collective-permute-start.11
  53.4 5.2 %collective-permute-done.7 = f32[8,2,32,128]{3,2,0,1:T(8,128)S(1)} collective-permute-done((f32[8,2,32,128]{3,2,0,1:T(8,128)S(1)}, f32[8,2,32,128]{3,2,0,1:T(8,128)S(1)}, u32[]{:S(2)}, u32[]{:S(2)}) %collective-permute-start.7) | collective-permute-done | bytes 262176 | tf_op jit(solution)/shard_map/ppermute | solution.py:29
  60.0 9.8 %collective-permute-done.11 = f32[8,2,32,128]{3,2,0,1:T(8,128)S(1)} collective-permute-done((f32[8,2,32,128]{3,2,0,1:T(8,128)S(1)}, f32[8,2,32,128]{3,2,0,1:T(8,128)S(1)}, u32[]{:S(2)}, u32[]{:S(2)}) %collective-permute-start.11) | collective-permute-done | bytes 262176 | tf_op jit(solution)/shard_map/ppermute | solution.py:29
  75.2 3.8 collective-permute-done.12
  81.1 4.0 %collective-permute-done.13 = f32[8,2,32,128]{3,2,0,1:T(8,128)S(1)} collective-permute-done((f32[8,2,32,128]{3,2,0,1:T(8,128)S(1)}, f32[8,2,32,128]{3,2,0,1:T(8,128)S(1)}, u32[]{:S(2)}, u32[]{:S(2)}) %collective-permute-start.13) | collective-permute-done | bytes 262176 | tf_op jit(solution)/shard_map/ppermute | solution.py:29
  89.3 2.8 collective-permute-done.10
  92.2 2.8 collective-permute-done.18
  95.0 2.3 fusion.25
  97.3 2.0 fusion.47
  101.6 4.0 %collective-permute-done.19 = f32[32,2,64,128]{3,2,0,1:T(8,128)} collective-permute-done((f32[32,2,64,128]{3,2,0,1:T(8,128)}, f32[32,2,64,128]{3,2,0,1:T(8,128)}, u32[]{:S(2)}, u32[]{:S(2)}) %collective-permute-start.19) | collective-permute-done | bytes 2097184 | tf_op jit(solution)/shard_map/ppermute | solution.py:29
  105.6 2.2 pad_maximum_fusion
  107.9 7.0 %fusion.37 = f32[64,128,256,1]{2,1,3,0:T(8,128)S(1)} fusion(f32[64,2,64,128]{3,2,0,1:T(8,128)S(1)} %pad_maximum_fusion, f32[64,1,256]{2,0,1:T(8,128)S(1)} %get-tuple-element.58, f32[64,1,256]{2,0,1:T(8,128)S(1)} %get-tuple-element.57), kind=kOutput, calls=%fused_computation.49 | convolution fusion | flops 1610645504 | bytes 12713984 | tf_op jit(solution)/shard_map/npxy,npz->xyz/dot_general | solution.py:24
  114.9 9.6 %fusion.2 = f32[2,8,2,64,128]{4,1,3,2,0:T(8,128)S(1)} fusion(f32[64,128,256]{2,1,0:T(8,128)} %param.3, f32[64,128,256,1]{2,1,3,0:T(8,128)S(1)} %fusion.37, f32[64,128,256]{2,1,0:T(8,128)S(1)} %bitcast.321, f32[2,8,1,256]{3,1,2,0:T(8,128)S(1)} %copy-done.4, f32[2,8,1,256]{3,1,2,0:T(8,128)S(1)} %get-tuple-element.71), kind=kOutput, calls=%fused_computation.2 | convolution fusion | flops 408952832 | bytes 26247168 | tf_op jit(solution)/shard_map/hkpz,xyz->hkpxy/dot_general | solution.py:24
  124.8 1.8 collective-permute-done.40
  131.7 5.6 %collective-permute-done.41 = f32[8,2,32,128]{3,2,0,1:T(8,128)S(1)} collective-permute-done((f32[8,2,32,128]{3,2,0,1:T(8,128)S(1)}, f32[8,2,32,128]{3,2,0,1:T(8,128)S(1)}, u32[]{:S(2)}, u32[]{:S(2)}) %collective-permute-start.41) | collective-permute-done | bytes 262176 | tf_op jit(solution)/shard_map/ppermute | solution.py:29
  137.3 6.1 %collective-permute-done.42 = f32[8,2,32,128]{3,2,0,1:T(8,128)S(1)} collective-permute-done((f32[8,2,32,128]{3,2,0,1:T(8,128)S(1)}, f32[8,2,32,128]{3,2,0,1:T(8,128)S(1)}, u32[]{:S(2)}, u32[]{:S(2)}) %collective-permute-start.42) | collective-permute-done | bytes 262176 | tf_op jit(solution)/shard_map/ppermute | solution.py:29
  143.6 3.4 collective-permute-start.27
  151.2 5.7 %collective-permute-done.27 = f32[8,2,32,128]{3,2,0,1:T(8,128)S(1)} collective-permute-done((f32[8,2,32,128]{3,2,0,1:T(8,128)S(1)}, f32[8,2,32,128]{3,2,0,1:T(8,128)S(1)}, u32[]{:S(2)}, u32[]{:S(2)}) %collective-permute-start.27) | collective-permute-done | bytes 262176 | tf_op jit(solution)/shard_map/ppermute | solution.py:29
  157.3 10.9 %collective-permute-done.31 = f32[8,2,32,128]{3,2,0,1:T(8,128)S(1)} collective-permute-done((f32[8,2,32,128]{3,2,0,1:T(8,128)S(1)}, f32[8,2,32,128]{3,2,0,1:T(8,128)S(1)}, u32[]{:S(2)}, u32[]{:S(2)}) %collective-permute-start.31) | collective-permute-done | bytes 262176 | tf_op jit(solution)/shard_map/ppermute | solution.py:29
  172.8 4.6 %collective-permute-done.32 = f32[8,2,32,128]{3,2,0,1:T(8,128)S(1)} collective-permute-done((f32[8,2,32,128]{3,2,0,1:T(8,128)S(1)}, f32[8,2,32,128]{3,2,0,1:T(8,128)S(1)}, u32[]{:S(2)}, u32[]{:S(2)}) %collective-permute-start.32) | collective-permute-done | bytes 262176 | tf_op jit(solution)/shard_map/ppermute | solution.py:29
  179.5 4.0 %collective-permute-done.26 = f32[8,2,32,128]{3,2,0,1:T(8,128)S(1)} collective-permute-done((f32[8,2,32,128]{3,2,0,1:T(8,128)S(1)}, f32[8,2,32,128]{3,2,0,1:T(8,128)S(1)}, u32[]{:S(2)}, u32[]{:S(2)}) %collective-permute-start.26) | collective-permute-done | bytes 262176 | tf_op jit(solution)/shard_map/ppermute | solution.py:29
  187.8 2.8 collective-permute-done.30
  193.5 7.3 %fusion.23 = f32[2,128,32,128,1]{3,1,0,4,2:T(8,128)S(1)} fusion(f32[1,128,2,128]{1,3,2,0:T(8,128)S(1)} %copy-done.13, f32[1,128,2,128]{1,3,2,0:T(8,128)S(1)} %copy-done.10, f32[8,2,32,128]{3,2,0,1:T(8,128)} %collective-permute-done.38, f32[8,2,32,128]{3,2,0,1:T(8,128)S(1)} %collective-permute-done.37, f32[8,2,32,128]{3,2,0,1:T(8,128)S(1)} %collective-permute-done.36, ...), kind=kOutput, calls=%fused_computation.35 | convolution fusion | flops 1627455488 | bytes 8650752 | tf_op jit(solution)/shard_map/npjm,pjqx->nqxm/dot_general | solution.py:24
  200.8 2.0 fusion.50
  203.2 4.1 %collective-permute-done.39 = f32[32,2,64,128]{3,2,0,1:T(8,128)S(1)} collective-permute-done((f32[32,2,64,128]{3,2,0,1:T(8,128)S(1)}, f32[32,2,64,128]{3,2,0,1:T(8,128)S(1)}, u32[]{:S(2)}, u32[]{:S(2)}) %collective-permute-start.39) | collective-permute-done | bytes 2097184 | tf_op jit(solution)/shard_map/ppermute | solution.py:29
  207.9 9.0 %fusion.35 = f32[64,128,256,1]{2,1,3,0:T(8,128)} fusion(f32[64,2,64,128]{3,2,0,1:T(8,128)S(1)} %pad_maximum_fusion.1, f32[64,1,256]{2,0,1:T(8,128)S(1)} %get-tuple-element.58, f32[64,1,256]{2,0,1:T(8,128)S(1)} %get-tuple-element.57), kind=kOutput, calls=%fused_computation.47 | convolution fusion | flops 1610645504 | bytes 12713984 | tf_op jit(solution)/shard_map/npxy,npz->xyz/dot_general | solution.py:24
  216.9 10.8 %fusion = f32[2,8,2,64,128]{4,1,3,2,0:T(8,128)S(1)} fusion(f32[64,128,256]{2,1,0:T(8,128)} %param.3, f32[64,128,256,1]{2,1,3,0:T(8,128)} %fusion.35, f32[64,128,256,1]{2,1,3,0:T(8,128)} %copy-done.1, f32[64,128,256]{2,1,0:T(8,128)S(1)} %bitcast.321, f32[2,8,1,256]{3,1,2,0:T(8,128)S(1)} %copy-done.4, f32[2,8,1,256]{3,1,2,0:T(8,128)S(1)} %get-tuple-element.71), kind=kOutput, calls=%fused_computation | convolution fusion | flops 413147136 | bytes 34635776 | tf_op jit(solution)/shard_map/hkpz,xyz->hkpxy/dot_general | solution.py:24
  234.9 5.6 %collective-permute-done.61 = f32[8,2,32,128]{3,2,0,1:T(8,128)S(1)} collective-permute-done((f32[8,2,32,128]{3,2,0,1:T(8,128)S(1)}, f32[8,2,32,128]{3,2,0,1:T(8,128)S(1)}, u32[]{:S(2)}, u32[]{:S(2)}) %collective-permute-start.61) | collective-permute-done | bytes 262176 | tf_op jit(solution)/shard_map/ppermute | solution.py:29
  240.4 5.1 %collective-permute-done.62 = f32[8,2,32,128]{3,2,0,1:T(8,128)S(1)} collective-permute-done((f32[8,2,32,128]{3,2,0,1:T(8,128)S(1)}, f32[8,2,32,128]{3,2,0,1:T(8,128)S(1)}, u32[]{:S(2)}, u32[]{:S(2)}) %collective-permute-start.62) | collective-permute-done | bytes 262176 | tf_op jit(solution)/shard_map/ppermute | solution.py:29
  245.9 3.4 collective-permute-start.67
  249.3 2.9 collective-permute-start.51
  255.1 6.9 %collective-permute-done.67 = f32[8,2,32,128]{3,2,0,1:T(8,128)S(1)} collective-permute-done((f32[8,2,32,128]{3,2,0,1:T(8,128)S(1)}, f32[8,2,32,128]{3,2,0,1:T(8,128)S(1)}, u32[]{:S(2)}, u32[]{:S(2)}) %collective-permute-start.67) | collective-permute-done | bytes 262176 | tf_op jit(solution)/shard_map/ppermute | solution.py:29
  263.7 2.2 collective-permute-done.47
  268.7 5.1 %collective-permute-done.55 = f32[8,2,32,128]{3,2,0,1:T(8,128)S(1)} collective-permute-done((f32[8,2,32,128]{3,2,0,1:T(8,128)S(1)}, f32[8,2,32,128]{3,2,0,1:T(8,128)S(1)}, u32[]{:S(2)}, u32[]{:S(2)}) %collective-permute-start.55) | collective-permute-done | bytes 262176 | tf_op jit(solution)/shard_map/ppermute | solution.py:29
  279.4 3.6 collective-permute-done.57
  284.7 3.9 %collective-permute-done.46 = f32[8,2,32,128]{3,2,0,1:T(8,128)S(1)} collective-permute-done((f32[8,2,32,128]{3,2,0,1:T(8,128)S(1)}, f32[8,2,32,128]{3,2,0,1:T(8,128)S(1)}, u32[]{:S(2)}, u32[]{:S(2)}) %collective-permute-start.46) | collective-permute-done | bytes 262176 | tf_op jit(solution)/shard_map/ppermute | solution.py:29
  290.7 3.4 collective-permute-done.53
  298.6 2.9 collective-permute-done.58
  302.5 2.3 fusion.21
  304.8 4.1 %collective-permute-done.71 = f32[8,2,32,128]{3,2,0,1:T(8,128)S(1)} collective-permute-done((f32[8,2,32,128]{3,2,0,1:T(8,128)S(1)}, f32[8,2,32,128]{3,2,0,1:T(8,128)S(1)}, u32[]{:S(2)}, u32[]{:S(2)}) %collective-permute-start.71) | collective-permute-done | bytes 262176 | tf_op jit(solution)/shard_map/ppermute | solution.py:29
  311.0 1.9 collective-permute-start.77
  313.0 2.0 fusion.53
  315.0 1.9 collective-permute-start.73
  316.9 5.8 %collective-permute-done.72 = f32[8,2,32,128]{3,2,0,1:T(8,128)S(1)} collective-permute-done((f32[8,2,32,128]{3,2,0,1:T(8,128)S(1)}, f32[8,2,32,128]{3,2,0,1:T(8,128)S(1)}, u32[]{:S(2)}, u32[]{:S(2)}) %collective-permute-start.72) | collective-permute-done | bytes 262176 | tf_op jit(solution)/shard_map/ppermute | solution.py:29
  325.8 1.9 collective-permute-start.74
  327.8 1.8 fusion.153
  329.6 1.8 collective-permute-done.73
  331.9 5.6 %collective-permute-done.70 = f32[8,2,32,128]{3,2,0,1:T(8,128)S(1)} collective-permute-done((f32[8,2,32,128]{3,2,0,1:T(8,128)S(1)}, f32[8,2,32,128]{3,2,0,1:T(8,128)S(1)}, u32[]{:S(2)}, u32[]{:S(2)}) %collective-permute-start.70) | collective-permute-done | bytes 262176 | tf_op jit(solution)/shard_map/ppermute | solution.py:29
  337.5 3.7 collective-permute-done.78
  341.2 2.3 fusion.19
  343.6 2.2 fusion.56
  345.8 2.3 fusion.151
  348.1 2.1 pad_maximum_fusion.2
  350.2 8.9 %fusion.33 = f32[64,128,256,1]{2,1,3,0:T(8,128)} fusion(f32[64,2,64,128]{3,2,0,1:T(8,128)S(1)} %pad_maximum_fusion.2, f32[64,1,256]{2,0,1:T(8,128)S(1)} %get-tuple-element.58, f32[64,1,256]{2,0,1:T(8,128)S(1)} %get-tuple-element.57), kind=kOutput, calls=%fused_computation.45 | convolution fusion | flops 1610645504 | bytes 12713984 | tf_op jit(solution)/shard_map/npxy,npz->xyz/dot_general | solution.py:24
  359.2 4.4 %pad_maximum_fusion.3 = f32[64,2,64,128]{3,2,0,1:T(8,128)} fusion(f32[32,2,64,128]{3,2,0,1:T(8,128)} %collective-permute-done.79, f32[32,2,64,128]{3,2,0,1:T(8,128)S(1)} %copy-done.2), kind=kLoop, calls=%fused_computation.30 | loop fusion | flops 1048576 | bytes 8388608 | tf_op jit(solution)/shard_map/concatenate | solution.py:132
  363.6 25.1 %fusion.10 = f32[1,64,128,256]{3,2,1,0:T(8,128)} fusion(f32[64,128,256]{2,1,0:T(8,128)} %param.3, f32[64,128,256,1]{2,1,3,0:T(8,128)} %fusion.33, f32[64,128,256]{2,1,0:T(8,128)} %param.2, f32[]{:T(128)S(6)} %select_n.172, f32[]{:T(128)S(6)} %select_n.171, f32[]{:T(128)S(6)} %select_n.169, f32[64,128,256,1]{2,1,3,0:T(8,128)} %copy-done.1, ...), kind=kOutput, calls=%fused_computation.11 | convolution fusion | flops 1642102784 | bytes 54657036 | tf_op jit(solution)/shard_map/npxy,npz->xyz/dot_general | solution.py:24
  (231 shorter events, 90.2 us)
Async XLA Ops:
  18.9 10.2 %collective-permute-start.1 = (f32[8,2,32,128]{3,2,0,1:T(8,128)S(1)}, f32[8,2,32,128]{3,2,0,1:T(8,128)S(1)}, u32[]{:S(2)}, u32[]{:S(2)}) collective-permute-start(f32[8,2,32,128]{3,2,0,1:T(8,128)S(1)} %get-tuple-element.30), channel_id=1, source_target_pairs={{0,1},{1,0},{2,3},{3,2},{4,5},{5,4},{6,7},{7,6},{8,9},{9,8},{10,11... | collective-permute-start | bytes 786440 | tf_op jit(solution)/shard_map/ppermute | solution.py:29
  21.9 14.8 %collective-permute-start.2 = (f32[8,2,32,128]{3,2,0,1:T(8,128)S(1)}, f32[8,2,32,128]{3,2,0,1:T(8,128)S(1)}, u32[]{:S(2)}, u32[]{:S(2)}) collective-permute-start(f32[8,2,32,128]{3,2,0,1:T(8,128)S(1)} %get-tuple-element.32), channel_id=1, source_target_pairs={{0,4},{2,6},{4,0},{6,2},{1,5},{3,7},{5,1},{7,3},{8,12},{10,14},{12... | collective-permute-start | bytes 786440 | tf_op jit(solution)/shard_map/ppermute | solution.py:29
  23.4 13.3 %collective-permute-start.3 = (f32[8,2,32,128]{3,2,0,1:T(8,128)S(1)}, f32[8,2,32,128]{3,2,0,1:T(8,128)S(1)}, u32[]{:S(2)}, u32[]{:S(2)}) collective-permute-start(f32[8,2,32,128]{3,2,0,1:T(8,128)S(1)} %get-tuple-element.31), channel_id=1, source_target_pairs={{0,5},{1,4},{2,7},{3,6},{4,1},{5,0},{6,3},{7,2},{8,13},{9,12},{10,... | collective-permute-start | bytes 786440 | tf_op jit(solution)/shard_map/ppermute | solution.py:29
  24.9 15.5 %collective-permute-start.21 = (f32[8,2,32,128]{3,2,0,1:T(8,128)S(1)}, f32[8,2,32,128]{3,2,0,1:T(8,128)S(1)}, u32[]{:S(2)}, u32[]{:S(2)}) collective-permute-start(f32[8,2,32,128]{3,2,0,1:T(8,128)S(1)} %get-tuple-element.20), channel_id=1, source_target_pairs={{0,1},{1,0},{2,3},{3,2},{4,5},{5,4},{6,7},{7,6},{8,9},{9,8},{10,11... | collective-permute-start | bytes 786440 | tf_op jit(solution)/shard_map/ppermute | solution.py:29
  26.9 19.8 %collective-permute-start.22 = (f32[8,2,32,128]{3,2,0,1:T(8,128)S(1)}, f32[8,2,32,128]{3,2,0,1:T(8,128)S(1)}, u32[]{:S(2)}, u32[]{:S(2)}) collective-permute-start(f32[8,2,32,128]{3,2,0,1:T(8,128)S(1)} %get-tuple-element.22), channel_id=1, source_target_pairs={{0,4},{2,6},{4,0},{6,2},{1,5},{3,7},{5,1},{7,3},{8,12},{10,14},{12... | collective-permute-start | bytes 786440 | tf_op jit(solution)/shard_map/ppermute | solution.py:29
  29.1 17.7 %collective-permute-start.23 = (f32[8,2,32,128]{3,2,0,1:T(8,128)S(1)}, f32[8,2,32,128]{3,2,0,1:T(8,128)S(1)}, u32[]{:S(2)}, u32[]{:S(2)}) collective-permute-start(f32[8,2,32,128]{3,2,0,1:T(8,128)S(1)} %get-tuple-element.21), channel_id=1, source_target_pairs={{0,5},{1,4},{2,7},{3,6},{4,1},{5,0},{6,3},{7,2},{8,13},{9,12},{10,... | collective-permute-start | bytes 786440 | tf_op jit(solution)/shard_map/ppermute | solution.py:29
  46.9 11.7 %collective-permute-start.7 = (f32[8,2,32,128]{3,2,0,1:T(8,128)S(1)}, f32[8,2,32,128]{3,2,0,1:T(8,128)S(1)}, u32[]{:S(2)}, u32[]{:S(2)}) collective-permute-start(f32[8,2,32,128]{3,2,0,1:T(8,128)S(1)} %get-tuple-element.48), channel_id=1, source_target_pairs={{0,8},{8,0},{16,24},{24,16},{1,9},{9,1},{17,25},{25,17},{2,10},{10... | collective-permute-start | bytes 786440 | tf_op jit(solution)/shard_map/ppermute | solution.py:29
  48.5 21.3 %collective-permute-start.11 = (f32[8,2,32,128]{3,2,0,1:T(8,128)S(1)}, f32[8,2,32,128]{3,2,0,1:T(8,128)S(1)}, u32[]{:S(2)}, u32[]{:S(2)}) collective-permute-start(f32[8,2,32,128]{3,2,0,1:T(8,128)S(1)} %get-tuple-element.48), channel_id=1, source_target_pairs={{0,16},{8,24},{16,0},{24,8},{1,17},{9,25},{17,1},{25,9},{2,18},{10... | collective-permute-start | bytes 786440 | tf_op jit(solution)/shard_map/ppermute | solution.py:29
  51.1 20.0 %collective-permute-start.15 = (f32[8,2,32,128]{3,2,0,1:T(8,128)S(1)}, f32[8,2,32,128]{3,2,0,1:T(8,128)S(1)}, u32[]{:S(2)}, u32[]{:S(2)}) collective-permute-start(f32[8,2,32,128]{3,2,0,1:T(8,128)S(1)} %get-tuple-element.48), channel_id=1, source_target_pairs={{0,24},{8,16},{16,8},{24,0},{1,25},{9,17},{17,9},{25,1},{2,26},{10... | collective-permute-start | bytes 786440 | tf_op jit(solution)/shard_map/ppermute | solution.py:29
  51.3 20.6 %collective-permute-start.4 = (f32[8,2,32,128]{3,2,0,1:T(8,128)S(1)}, f32[8,2,32,128]{3,2,0,1:T(8,128)S(1)}, u32[]{:S(2)}, u32[]{:S(2)}) collective-permute-start(f32[8,2,32,128]{3,2,0,1:T(8,128)S(1)} %get-tuple-element.48), channel_id=1, source_target_pairs={{0,1},{1,0},{2,3},{3,2},{4,5},{5,4},{6,7},{7,6},{8,9},{9,8},{10,11... | collective-permute-start | bytes 786440 | tf_op jit(solution)/shard_map/ppermute | solution.py:29
  52.6 20.5 %collective-permute-start.5 = (f32[8,2,32,128]{3,2,0,1:T(8,128)S(1)}, f32[8,2,32,128]{3,2,0,1:T(8,128)S(1)}, u32[]{:S(2)}, u32[]{:S(2)}) collective-permute-start(f32[8,2,32,128]{3,2,0,1:T(8,128)S(1)} %get-tuple-element.48), channel_id=1, source_target_pairs={{0,4},{2,6},{4,0},{6,2},{1,5},{3,7},{5,1},{7,3},{8,12},{10,14},{12... | collective-permute-start | bytes 786440 | tf_op jit(solution)/shard_map/ppermute | solution.py:29
  58.6 15.3 %collective-permute-start.9 = (f32[8,2,32,128]{3,2,0,1:T(8,128)S(1)}, f32[8,2,32,128]{3,2,0,1:T(8,128)S(1)}, u32[]{:S(2)}, u32[]{:S(2)}) collective-permute-start(f32[8,2,32,128]{3,2,0,1:T(8,128)S(1)} %collective-permute-done.7), channel_id=1, source_target_pairs={{0,4},{2,6},{4,0},{6,2},{1,5},{3,7},{5,1},{7,3},{8,12},{10,14},{12... | collective-permute-start | bytes 786440 | tf_op jit(solution)/shard_map/ppermute | solution.py:29
  71.9 13.2 %collective-permute-start.13 = (f32[8,2,32,128]{3,2,0,1:T(8,128)S(1)}, f32[8,2,32,128]{3,2,0,1:T(8,128)S(1)}, u32[]{:S(2)}, u32[]{:S(2)}) collective-permute-start(f32[8,2,32,128]{3,2,0,1:T(8,128)S(1)} %collective-permute-done.11), channel_id=1, source_target_pairs={{0,4},{2,6},{4,0},{6,2},{1,5},{3,7},{5,1},{7,3},{8,12},{10,14},{12... | collective-permute-start | bytes 786440 | tf_op jit(solution)/shard_map/ppermute | solution.py:29
  73.2 12.2 %collective-permute-start.16 = (f32[8,2,32,128]{3,2,0,1:T(8,128)S(1)}, f32[8,2,32,128]{3,2,0,1:T(8,128)S(1)}, u32[]{:S(2)}, u32[]{:S(2)}) collective-permute-start(f32[8,2,32,128]{3,2,0,1:T(8,128)S(1)} %collective-permute-done.15), channel_id=1, source_target_pairs={{0,1},{1,0},{2,3},{3,2},{4,5},{5,4},{6,7},{7,6},{8,9},{9,8},{10,11... | collective-permute-start | bytes 786440 | tf_op jit(solution)/shard_map/ppermute | solution.py:29
  73.9 15.5 %collective-permute-start.8 = (f32[8,2,32,128]{3,2,0,1:T(8,128)S(1)}, f32[8,2,32,128]{3,2,0,1:T(8,128)S(1)}, u32[]{:S(2)}, u32[]{:S(2)}) collective-permute-start(f32[8,2,32,128]{3,2,0,1:T(8,128)S(1)} %collective-permute-done.7), channel_id=1, source_target_pairs={{0,1},{1,0},{2,3},{3,2},{4,5},{5,4},{6,7},{7,6},{8,9},{9,8},{10,11... | collective-permute-start | bytes 786440 | tf_op jit(solution)/shard_map/ppermute | solution.py:29
  80.3 11.9 %collective-permute-start.10 = (f32[8,2,32,128]{3,2,0,1:T(8,128)S(1)}, f32[8,2,32,128]{3,2,0,1:T(8,128)S(1)}, u32[]{:S(2)}, u32[]{:S(2)}) collective-permute-start(f32[8,2,32,128]{3,2,0,1:T(8,128)S(1)} %collective-permute-done.9), channel_id=1, source_target_pairs={{0,1},{1,0},{2,3},{3,2},{4,5},{5,4},{6,7},{7,6},{8,9},{9,8},{10,11... | collective-permute-start | bytes 786440 | tf_op jit(solution)/shard_map/ppermute | solution.py:29
  85.4 9.6 %collective-permute-start.18 = (f32[8,2,32,128]{3,2,0,1:T(8,128)S(1)}, f32[8,2,32,128]{3,2,0,1:T(8,128)S(1)}, u32[]{:S(2)}, u32[]{:S(2)}) collective-permute-start(f32[8,2,32,128]{3,2,0,1:T(8,128)S(1)} %collective-permute-done.17), channel_id=1, source_target_pairs={{0,1},{1,0},{2,3},{3,2},{4,5},{5,4},{6,7},{7,6},{8,9},{9,8},{10,11... | collective-permute-start | bytes 786440 | tf_op jit(solution)/shard_map/ppermute | solution.py:29
  128.1 9.2 %collective-permute-start.41 = (f32[8,2,32,128]{3,2,0,1:T(8,128)S(1)}, f32[8,2,32,128]{3,2,0,1:T(8,128)S(1)}, u32[]{:S(2)}, u32[]{:S(2)}) collective-permute-start(f32[8,2,32,128]{3,2,0,1:T(8,128)S(1)} %get-tuple-element.25), channel_id=1, source_target_pairs={{0,1},{1,0},{2,3},{3,2},{4,5},{5,4},{6,7},{7,6},{8,9},{9,8},{10,11... | collective-permute-start | bytes 786440 | tf_op jit(solution)/shard_map/ppermute | solution.py:29
  129.7 13.7 %collective-permute-start.42 = (f32[8,2,32,128]{3,2,0,1:T(8,128)S(1)}, f32[8,2,32,128]{3,2,0,1:T(8,128)S(1)}, u32[]{:S(2)}, u32[]{:S(2)}) collective-permute-start(f32[8,2,32,128]{3,2,0,1:T(8,128)S(1)} %get-tuple-element.27), channel_id=1, source_target_pairs={{0,4},{2,6},{4,0},{6,2},{1,5},{3,7},{5,1},{7,3},{8,12},{10,14},{12... | collective-permute-start | bytes 786440 | tf_op jit(solution)/shard_map/ppermute | solution.py:29
  130.1 13.3 %collective-permute-start.43 = (f32[8,2,32,128]{3,2,0,1:T(8,128)S(1)}, f32[8,2,32,128]{3,2,0,1:T(8,128)S(1)}, u32[]{:S(2)}, u32[]{:S(2)}) collective-permute-start(f32[8,2,32,128]{3,2,0,1:T(8,128)S(1)} %get-tuple-element.26), channel_id=1, source_target_pairs={{0,5},{1,4},{2,7},{3,6},{4,1},{5,0},{6,3},{7,2},{8,13},{9,12},{10,... | collective-permute-start | bytes 786440 | tf_op jit(solution)/shard_map/ppermute | solution.py:29
  143.6 13.3 %collective-permute-start.27 = (f32[8,2,32,128]{3,2,0,1:T(8,128)S(1)}, f32[8,2,32,128]{3,2,0,1:T(8,128)S(1)}, u32[]{:S(2)}, u32[]{:S(2)}) collective-permute-start(f32[8,2,32,128]{3,2,0,1:T(8,128)S(1)} %get-tuple-element.45), channel_id=1, source_target_pairs={{0,8},{8,0},{16,24},{24,16},{1,9},{9,1},{17,25},{25,17},{2,10},{10... | collective-permute-start | bytes 786440 | tf_op jit(solution)/shard_map/ppermute | solution.py:29
  147.0 21.3 %collective-permute-start.31 = (f32[8,2,32,128]{3,2,0,1:T(8,128)S(1)}, f32[8,2,32,128]{3,2,0,1:T(8,128)S(1)}, u32[]{:S(2)}, u32[]{:S(2)}) collective-permute-start(f32[8,2,32,128]{3,2,0,1:T(8,128)S(1)} %get-tuple-element.45), channel_id=1, source_target_pairs={{0,16},{8,24},{16,0},{24,8},{1,17},{9,25},{17,1},{25,9},{2,18},{10... | collective-permute-start | bytes 786440 | tf_op jit(solution)/shard_map/ppermute | solution.py:29
  148.0 20.7 %collective-permute-start.35 = (f32[8,2,32,128]{3,2,0,1:T(8,128)S(1)}, f32[8,2,32,128]{3,2,0,1:T(8,128)S(1)}, u32[]{:S(2)}, u32[]{:S(2)}) collective-permute-start(f32[8,2,32,128]{3,2,0,1:T(8,128)S(1)} %get-tuple-element.45), channel_id=1, source_target_pairs={{0,24},{8,16},{16,8},{24,0},{1,25},{9,17},{17,9},{25,1},{2,26},{10... | collective-permute-start | bytes 786440 | tf_op jit(solution)/shard_map/ppermute | solution.py:29
  149.4 20.6 %collective-permute-start.24 = (f32[8,2,32,128]{3,2,0,1:T(8,128)S(1)}, f32[8,2,32,128]{3,2,0,1:T(8,128)S(1)}, u32[]{:S(2)}, u32[]{:S(2)}) collective-permute-start(f32[8,2,32,128]{3,2,0,1:T(8,128)S(1)} %get-tuple-element.45), channel_id=1, source_target_pairs={{0,1},{1,0},{2,3},{3,2},{4,5},{5,4},{6,7},{7,6},{8,9},{9,8},{10,11... | collective-permute-start | bytes 786440 | tf_op jit(solution)/shard_map/ppermute | solution.py:29
  149.9 20.9 %collective-permute-start.25 = (f32[8,2,32,128]{3,2,0,1:T(8,128)S(1)}, f32[8,2,32,128]{3,2,0,1:T(8,128)S(1)}, u32[]{:S(2)}, u32[]{:S(2)}) collective-permute-start(f32[8,2,32,128]{3,2,0,1:T(8,128)S(1)} %get-tuple-element.45), channel_id=1, source_target_pairs={{0,4},{2,6},{4,0},{6,2},{1,5},{3,7},{5,1},{7,3},{8,12},{10,14},{12... | collective-permute-start | bytes 786440 | tf_op jit(solution)/shard_map/ppermute | solution.py:29
  156.9 15.5 %collective-permute-start.29 = (f32[8,2,32,128]{3,2,0,1:T(8,128)S(1)}, f32[8,2,32,128]{3,2,0,1:T(8,128)S(1)}, u32[]{:S(2)}, u32[]{:S(2)}) collective-permute-start(f32[8,2,32,128]{3,2,0,1:T(8,128)S(1)} %collective-permute-done.27), channel_id=1, source_target_pairs={{0,4},{2,6},{4,0},{6,2},{1,5},{3,7},{5,1},{7,3},{8,12},{10,14},{12... | collective-permute-start | bytes 786440 | tf_op jit(solution)/shard_map/ppermute | solution.py:29
  170.0 13.5 %collective-permute-start.26 = (f32[8,2,32,128]{3,2,0,1:T(8,128)S(1)}, f32[8,2,32,128]{3,2,0,1:T(8,128)S(1)}, u32[]{:S(2)}, u32[]{:S(2)}) collective-permute-start(f32[8,2,32,128]{3,2,0,1:T(8,128)S(1)} %collective-permute-done.24), channel_id=1, source_target_pairs={{0,4},{2,6},{4,0},{6,2},{1,5},{3,7},{5,1},{7,3},{8,12},{10,14},{12... | collective-permute-start | bytes 786440 | tf_op jit(solution)/shard_map/ppermute | solution.py:29
  170.8 13.2 %collective-permute-start.28 = (f32[8,2,32,128]{3,2,0,1:T(8,128)S(1)}, f32[8,2,32,128]{3,2,0,1:T(8,128)S(1)}, u32[]{:S(2)}, u32[]{:S(2)}) collective-permute-start(f32[8,2,32,128]{3,2,0,1:T(8,128)S(1)} %collective-permute-done.27), channel_id=1, source_target_pairs={{0,1},{1,0},{2,3},{3,2},{4,5},{5,4},{6,7},{7,6},{8,9},{9,8},{10,11... | collective-permute-start | bytes 786440 | tf_op jit(solution)/shard_map/ppermute | solution.py:29
  172.3 13.9 %collective-permute-start.33 = (f32[8,2,32,128]{3,2,0,1:T(8,128)S(1)}, f32[8,2,32,128]{3,2,0,1:T(8,128)S(1)}, u32[]{:S(2)}, u32[]{:S(2)}) collective-permute-start(f32[8,2,32,128]{3,2,0,1:T(8,128)S(1)} %collective-permute-done.31), channel_id=1, source_target_pairs={{0,4},{2,6},{4,0},{6,2},{1,5},{3,7},{5,1},{7,3},{8,12},{10,14},{12... | collective-permute-start | bytes 786440 | tf_op jit(solution)/shard_map/ppermute | solution.py:29
  177.5 10.3 %collective-permute-start.36 = (f32[8,2,32,128]{3,2,0,1:T(8,128)S(1)}, f32[8,2,32,128]{3,2,0,1:T(8,128)S(1)}, u32[]{:S(2)}, u32[]{:S(2)}) collective-permute-start(f32[8,2,32,128]{3,2,0,1:T(8,128)S(1)} %collective-permute-done.35), channel_id=1, source_target_pairs={{0,1},{1,0},{2,3},{3,2},{4,5},{5,4},{6,7},{7,6},{8,9},{9,8},{10,11... | collective-permute-start | bytes 786440 | tf_op jit(solution)/shard_map/ppermute | solution.py:29
  177.9 12.7 %collective-permute-start.30 = (f32[8,2,32,128]{3,2,0,1:T(8,128)S(1)}, f32[8,2,32,128]{3,2,0,1:T(8,128)S(1)}, u32[]{:S(2)}, u32[]{:S(2)}) collective-permute-start(f32[8,2,32,128]{3,2,0,1:T(8,128)S(1)} %collective-permute-done.29), channel_id=1, source_target_pairs={{0,1},{1,0},{2,3},{3,2},{4,5},{5,4},{6,7},{7,6},{8,9},{9,8},{10,11... | collective-permute-start | bytes 786440 | tf_op jit(solution)/shard_map/ppermute | solution.py:29
  184.0 9.5 %collective-permute-start.38 = (f32[8,2,32,128]{3,2,0,1:T(8,128)S(1)}, f32[8,2,32,128]{3,2,0,1:T(8,128)}, u32[]{:S(2)}, u32[]{:S(2)}) collective-permute-start(f32[8,2,32,128]{3,2,0,1:T(8,128)S(1)} %collective-permute-done.37), channel_id=1, source_target_pairs={{0,1},{1,0},{2,3},{3,2},{4,5},{5,4},{6,7},{7,6},{8,9},{9,8},{10,11... | collective-permute-start | bytes 786440 | tf_op jit(solution)/shard_map/ppermute | solution.py:29
  231.9 13.7 %collective-permute-start.62 = (f32[8,2,32,128]{3,2,0,1:T(8,128)S(1)}, f32[8,2,32,128]{3,2,0,1:T(8,128)S(1)}, u32[]{:S(2)}, u32[]{:S(2)}) collective-permute-start(f32[8,2,32,128]{3,2,0,1:T(8,128)S(1)} %get-tuple-element.17), channel_id=1, source_target_pairs={{0,4},{2,6},{4,0},{6,2},{1,5},{3,7},{5,1},{7,3},{8,12},{10,14},{12... | collective-permute-start | bytes 786440 | tf_op jit(solution)/shard_map/ppermute | solution.py:29
  233.6 12.0 %collective-permute-start.63 = (f32[8,2,32,128]{3,2,0,1:T(8,128)S(1)}, f32[8,2,32,128]{3,2,0,1:T(8,128)S(1)}, u32[]{:S(2)}, u32[]{:S(2)}) collective-permute-start(f32[8,2,32,128]{3,2,0,1:T(8,128)S(1)} %get-tuple-element.16), channel_id=1, source_target_pairs={{0,5},{1,4},{2,7},{3,6},{4,1},{5,0},{6,3},{7,2},{8,13},{9,12},{10,... | collective-permute-start | bytes 786440 | tf_op jit(solution)/shard_map/ppermute | solution.py:29
  245.9 16.2 %collective-permute-start.67 = (f32[8,2,32,128]{3,2,0,1:T(8,128)S(1)}, f32[8,2,32,128]{3,2,0,1:T(8,128)S(1)}, u32[]{:S(2)}, u32[]{:S(2)}) collective-permute-start(f32[8,2,32,128]{3,2,0,1:T(8,128)S(1)} %pad_maximum_fusion.7), channel_id=1, source_target_pairs={{0,8},{8,0},{16,24},{24,16},{1,9},{9,1},{17,25},{25,17},{2,10},{10... | collective-permute-start | bytes 786440 | tf_op jit(solution)/shard_map/ppermute | solution.py:29
  249.3 16.7 %collective-permute-start.47 = (f32[8,2,32,128]{3,2,0,1:T(8,128)S(1)}, f32[8,2,32,128]{3,2,0,1:T(8,128)S(1)}, u32[]{:S(2)}, u32[]{:S(2)}) collective-permute-start(f32[8,2,32,128]{3,2,0,1:T(8,128)S(1)} %get-tuple-element.44), channel_id=1, source_target_pairs={{0,8},{8,0},{16,24},{24,16},{1,9},{9,1},{17,25},{25,17},{2,10},{10... | collective-permute-start | bytes 786440 | tf_op jit(solution)/shard_map/ppermute | solution.py:29
  249.3 18.1 %collective-permute-start.51 = (f32[8,2,32,128]{3,2,0,1:T(8,128)S(1)}, f32[8,2,32,128]{3,2,0,1:T(8,128)S(1)}, u32[]{:S(2)}, u32[]{:S(2)}) collective-permute-start(f32[8,2,32,128]{3,2,0,1:T(8,128)S(1)} %get-tuple-element.44), channel_id=1, source_target_pairs={{0,16},{8,24},{16,0},{24,8},{1,17},{9,25},{17,1},{25,9},{2,18},{10... | collective-permute-start | bytes 786440 | tf_op jit(solution)/shard_map/ppermute | solution.py:29
  252.3 21.6 %collective-permute-start.55 = (f32[8,2,32,128]{3,2,0,1:T(8,128)S(1)}, f32[8,2,32,128]{3,2,0,1:T(8,128)S(1)}, u32[]{:S(2)}, u32[]{:S(2)}) collective-permute-start(f32[8,2,32,128]{3,2,0,1:T(8,128)S(1)} %get-tuple-element.44), channel_id=1, source_target_pairs={{0,24},{8,16},{16,8},{24,0},{1,25},{9,17},{17,9},{25,1},{2,26},{10... | collective-permute-start | bytes 786440 | tf_op jit(solution)/shard_map/ppermute | solution.py:29
  253.6 21.7 %collective-permute-start.44 = (f32[8,2,32,128]{3,2,0,1:T(8,128)S(1)}, f32[8,2,32,128]{3,2,0,1:T(8,128)S(1)}, u32[]{:S(2)}, u32[]{:S(2)}) collective-permute-start(f32[8,2,32,128]{3,2,0,1:T(8,128)S(1)} %get-tuple-element.44), channel_id=1, source_target_pairs={{0,1},{1,0},{2,3},{3,2},{4,5},{5,4},{6,7},{7,6},{8,9},{9,8},{10,11... | collective-permute-start | bytes 786440 | tf_op jit(solution)/shard_map/ppermute | solution.py:29
  262.0 13.8 %collective-permute-start.45 = (f32[8,2,32,128]{3,2,0,1:T(8,128)S(1)}, f32[8,2,32,128]{3,2,0,1:T(8,128)S(1)}, u32[]{:S(2)}, u32[]{:S(2)}) collective-permute-start(f32[8,2,32,128]{3,2,0,1:T(8,128)S(1)} %get-tuple-element.44), channel_id=1, source_target_pairs={{0,4},{2,6},{4,0},{6,2},{1,5},{3,7},{5,1},{7,3},{8,12},{10,14},{12... | collective-permute-start | bytes 786440 | tf_op jit(solution)/shard_map/ppermute | solution.py:29
  265.9 11.6 %collective-permute-start.49 = (f32[8,2,32,128]{3,2,0,1:T(8,128)S(1)}, f32[8,2,32,128]{3,2,0,1:T(8,128)S(1)}, u32[]{:S(2)}, u32[]{:S(2)}) collective-permute-start(f32[8,2,32,128]{3,2,0,1:T(8,128)S(1)} %collective-permute-done.47), channel_id=1, source_target_pairs={{0,4},{2,6},{4,0},{6,2},{1,5},{3,7},{5,1},{7,3},{8,12},{10,14},{12... | collective-permute-start | bytes 786440 | tf_op jit(solution)/shard_map/ppermute | solution.py:29
  267.5 10.5 %collective-permute-start.52 = (f32[8,2,32,128]{3,2,0,1:T(8,128)S(1)}, f32[8,2,32,128]{3,2,0,1:T(8,128)S(1)}, u32[]{:S(2)}, u32[]{:S(2)}) collective-permute-start(f32[8,2,32,128]{3,2,0,1:T(8,128)S(1)} %collective-permute-done.51), channel_id=1, source_target_pairs={{0,1},{1,0},{2,3},{3,2},{4,5},{5,4},{6,7},{7,6},{8,9},{9,8},{10,11... | collective-permute-start | bytes 786440 | tf_op jit(solution)/shard_map/ppermute | solution.py:29
  275.3 13.3 %collective-permute-start.46 = (f32[8,2,32,128]{3,2,0,1:T(8,128)S(1)}, f32[8,2,32,128]{3,2,0,1:T(8,128)S(1)}, u32[]{:S(2)}, u32[]{:S(2)}) collective-permute-start(f32[8,2,32,128]{3,2,0,1:T(8,128)S(1)} %collective-permute-done.44), channel_id=1, source_target_pairs={{0,4},{2,6},{4,0},{6,2},{1,5},{3,7},{5,1},{7,3},{8,12},{10,14},{12... | collective-permute-start | bytes 786440 | tf_op jit(solution)/shard_map/ppermute | solution.py:29
  275.9 14.2 %collective-permute-start.48 = (f32[8,2,32,128]{3,2,0,1:T(8,128)S(1)}, f32[8,2,32,128]{3,2,0,1:T(8,128)S(1)}, u32[]{:S(2)}, u32[]{:S(2)}) collective-permute-start(f32[8,2,32,128]{3,2,0,1:T(8,128)S(1)} %collective-permute-done.47), channel_id=1, source_target_pairs={{0,1},{1,0},{2,3},{3,2},{4,5},{5,4},{6,7},{7,6},{8,9},{9,8},{10,11... | collective-permute-start | bytes 786440 | tf_op jit(solution)/shard_map/ppermute | solution.py:29
  277.6 16.6 %collective-permute-start.53 = (f32[8,2,32,128]{3,2,0,1:T(8,128)S(1)}, f32[8,2,32,128]{3,2,0,1:T(8,128)S(1)}, u32[]{:S(2)}, u32[]{:S(2)}) collective-permute-start(f32[8,2,32,128]{3,2,0,1:T(8,128)S(1)} %collective-permute-done.51), channel_id=1, source_target_pairs={{0,4},{2,6},{4,0},{6,2},{1,5},{3,7},{5,1},{7,3},{8,12},{10,14},{12... | collective-permute-start | bytes 786440 | tf_op jit(solution)/shard_map/ppermute | solution.py:29
  278.0 16.3 %collective-permute-start.56 = (f32[8,2,32,128]{3,2,0,1:T(8,128)S(1)}, f32[8,2,32,128]{3,2,0,1:T(8,128)S(1)}, u32[]{:S(2)}, u32[]{:S(2)}) collective-permute-start(f32[8,2,32,128]{3,2,0,1:T(8,128)S(1)} %collective-permute-done.55), channel_id=1, source_target_pairs={{0,1},{1,0},{2,3},{3,2},{4,5},{5,4},{6,7},{7,6},{8,9},{9,8},{10,11... | collective-permute-start | bytes 786440 | tf_op jit(solution)/shard_map/ppermute | solution.py:29
  283.0 13.3 %collective-permute-start.50 = (f32[8,2,32,128]{3,2,0,1:T(8,128)S(1)}, f32[8,2,32,128]{3,2,0,1:T(8,128)S(1)}, u32[]{:S(2)}, u32[]{:S(2)}) collective-permute-start(f32[8,2,32,128]{3,2,0,1:T(8,128)S(1)} %collective-permute-done.49), channel_id=1, source_target_pairs={{0,1},{1,0},{2,3},{3,2},{4,5},{5,4},{6,7},{7,6},{8,9},{9,8},{10,11... | collective-permute-start | bytes 786440 | tf_op jit(solution)/shard_map/ppermute | solution.py:29
  288.6 9.4 %collective-permute-start.54 = (f32[8,2,32,128]{3,2,0,1:T(8,128)S(1)}, f32[8,2,32,128]{3,2,0,1:T(8,128)S(1)}, u32[]{:S(2)}, u32[]{:S(2)}) collective-permute-start(f32[8,2,32,128]{3,2,0,1:T(8,128)S(1)} %collective-permute-done.52), channel_id=1, source_target_pairs={{0,4},{2,6},{4,0},{6,2},{1,5},{3,7},{5,1},{7,3},{8,12},{10,14},{12... | collective-permute-start | bytes 786440 | tf_op jit(solution)/shard_map/ppermute | solution.py:29
  290.1 11.4 %collective-permute-start.58 = (f32[8,2,32,128]{3,2,0,1:T(8,128)S(1)}, f32[8,2,32,128]{3,2,0,1:T(8,128)S(1)}, u32[]{:S(2)}, u32[]{:S(2)}) collective-permute-start(f32[8,2,32,128]{3,2,0,1:T(8,128)S(1)} %collective-permute-done.57), channel_id=1, source_target_pairs={{0,1},{1,0},{2,3},{3,2},{4,5},{5,4},{6,7},{7,6},{8,9},{9,8},{10,11... | collective-permute-start | bytes 786440 | tf_op jit(solution)/shard_map/ppermute | solution.py:29
  294.2 14.8 %collective-permute-start.71 = (f32[8,2,32,128]{3,2,0,1:T(8,128)S(1)}, f32[8,2,32,128]{3,2,0,1:T(8,128)S(1)}, u32[]{:S(2)}, u32[]{:S(2)}) collective-permute-start(f32[8,2,32,128]{3,2,0,1:T(8,128)S(1)} %pad_maximum_fusion.7), channel_id=1, source_target_pairs={{0,16},{8,24},{16,0},{24,8},{1,17},{9,25},{17,1},{25,9},{2,18},{10... | collective-permute-start | bytes 786440 | tf_op jit(solution)/shard_map/ppermute | solution.py:29
  294.2 15.9 %collective-permute-start.75 = (f32[8,2,32,128]{3,2,0,1:T(8,128)S(1)}, f32[8,2,32,128]{3,2,0,1:T(8,128)S(1)}, u32[]{:S(2)}, u32[]{:S(2)}) collective-permute-start(f32[8,2,32,128]{3,2,0,1:T(8,128)S(1)} %pad_maximum_fusion.7), channel_id=1, source_target_pairs={{0,24},{8,16},{16,8},{24,0},{1,25},{9,17},{17,9},{25,1},{2,26},{10... | collective-permute-start | bytes 786440 | tf_op jit(solution)/shard_map/ppermute | solution.py:29
  296.3 14.7 %collective-permute-start.64 = (f32[8,2,32,128]{3,2,0,1:T(8,128)S(1)}, f32[8,2,32,128]{3,2,0,1:T(8,128)S(1)}, u32[]{:S(2)}, u32[]{:S(2)}) collective-permute-start(f32[8,2,32,128]{3,2,0,1:T(8,128)S(1)} %pad_maximum_fusion.7), channel_id=1, source_target_pairs={{0,1},{1,0},{2,3},{3,2},{4,5},{5,4},{6,7},{7,6},{8,9},{9,8},{10,11... | collective-permute-start | bytes 786440 | tf_op jit(solution)/shard_map/ppermute | solution.py:29
  298.0 14.9 %collective-permute-start.65 = (f32[8,2,32,128]{3,2,0,1:T(8,128)S(1)}, f32[8,2,32,128]{3,2,0,1:T(8,128)S(1)}, u32[]{:S(2)}, u32[]{:S(2)}) collective-permute-start(f32[8,2,32,128]{3,2,0,1:T(8,128)S(1)} %pad_maximum_fusion.7), channel_id=1, source_target_pairs={{0,4},{2,6},{4,0},{6,2},{1,5},{3,7},{5,1},{7,3},{8,12},{10,14},{12... | collective-permute-start | bytes 786440 | tf_op jit(solution)/shard_map/ppermute | solution.py:29
  301.5 13.5 %collective-permute-start.69 = (f32[8,2,32,128]{3,2,0,1:T(8,128)S(1)}, f32[8,2,32,128]{3,2,0,1:T(8,128)S(1)}, u32[]{:S(2)}, u32[]{:S(2)}) collective-permute-start(f32[8,2,32,128]{3,2,0,1:T(8,128)S(1)} %collective-permute-done.67), channel_id=1, source_target_pairs={{0,4},{2,6},{4,0},{6,2},{1,5},{3,7},{5,1},{7,3},{8,12},{10,14},{12... | collective-permute-start | bytes 786440 | tf_op jit(solution)/shard_map/ppermute | solution.py:29
  309.0 18.7 %collective-permute-start.68 = (f32[8,2,32,128]{3,2,0,1:T(8,128)S(1)}, f32[8,2,32,128]{3,2,0,1:T(8,128)S(1)}, u32[]{:S(2)}, u32[]{:S(2)}) collective-permute-start(f32[8,2,32,128]{3,2,0,1:T(8,128)S(1)} %collective-permute-done.67), channel_id=1, source_target_pairs={{0,1},{1,0},{2,3},{3,2},{4,5},{5,4},{6,7},{7,6},{8,9},{9,8},{10,11... | collective-permute-start | bytes 786440 | tf_op jit(solution)/shard_map/ppermute | solution.py:29
  310.1 12.6 %collective-permute-start.72 = (f32[8,2,32,128]{3,2,0,1:T(8,128)S(1)}, f32[8,2,32,128]{3,2,0,1:T(8,128)S(1)}, u32[]{:S(2)}, u32[]{:S(2)}) collective-permute-start(f32[8,2,32,128]{3,2,0,1:T(8,128)S(1)} %collective-permute-done.71), channel_id=1, source_target_pairs={{0,1},{1,0},{2,3},{3,2},{4,5},{5,4},{6,7},{7,6},{8,9},{9,8},{10,11... | collective-permute-start | bytes 786440 | tf_op jit(solution)/shard_map/ppermute | solution.py:29
  311.0 12.8 %collective-permute-start.77 = (f32[8,2,32,128]{3,2,0,1:T(8,128)S(1)}, f32[8,2,32,128]{3,2,0,1:T(8,128)S(1)}, u32[]{:S(2)}, u32[]{:S(2)}) collective-permute-start(f32[8,2,32,128]{3,2,0,1:T(8,128)S(1)} %collective-permute-done.75), channel_id=1, source_target_pairs={{0,4},{2,6},{4,0},{6,2},{1,5},{3,7},{5,1},{7,3},{8,12},{10,14},{12... | collective-permute-start | bytes 786440 | tf_op jit(solution)/shard_map/ppermute | solution.py:29
  312.9 12.9 %collective-permute-start.66 = (f32[8,2,32,128]{3,2,0,1:T(8,128)S(1)}, f32[8,2,32,128]{3,2,0,1:T(8,128)S(1)}, u32[]{:S(2)}, u32[]{:S(2)}) collective-permute-start(f32[8,2,32,128]{3,2,0,1:T(8,128)S(1)} %collective-permute-done.64), channel_id=1, source_target_pairs={{0,4},{2,6},{4,0},{6,2},{1,5},{3,7},{5,1},{7,3},{8,12},{10,14},{12... | collective-permute-start | bytes 786440 | tf_op jit(solution)/shard_map/ppermute | solution.py:29
  315.0 16.4 %collective-permute-start.73 = (f32[8,2,32,128]{3,2,0,1:T(8,128)S(1)}, f32[8,2,32,128]{3,2,0,1:T(8,128)S(1)}, u32[]{:S(2)}, u32[]{:S(2)}) collective-permute-start(f32[8,2,32,128]{3,2,0,1:T(8,128)S(1)} %collective-permute-done.71), channel_id=1, source_target_pairs={{0,4},{2,6},{4,0},{6,2},{1,5},{3,7},{5,1},{7,3},{8,12},{10,14},{12... | collective-permute-start | bytes 786440 | tf_op jit(solution)/shard_map/ppermute | solution.py:29
  323.8 13.7 %collective-permute-start.70 = (f32[8,2,32,128]{3,2,0,1:T(8,128)S(1)}, f32[8,2,32,128]{3,2,0,1:T(8,128)S(1)}, u32[]{:S(2)}, u32[]{:S(2)}) collective-permute-start(f32[8,2,32,128]{3,2,0,1:T(8,128)S(1)} %collective-permute-done.69), channel_id=1, source_target_pairs={{0,1},{1,0},{2,3},{3,2},{4,5},{5,4},{6,7},{7,6},{8,9},{9,8},{10,11... | collective-permute-start | bytes 786440 | tf_op jit(solution)/shard_map/ppermute | solution.py:29
  325.8 11.7 %collective-permute-start.74 = (f32[8,2,32,128]{3,2,0,1:T(8,128)S(1)}, f32[8,2,32,128]{3,2,0,1:T(8,128)S(1)}, u32[]{:S(2)}, u32[]{:S(2)}) collective-permute-start(f32[8,2,32,128]{3,2,0,1:T(8,128)S(1)} %collective-permute-done.72), channel_id=1, source_target_pairs={{0,4},{2,6},{4,0},{6,2},{1,5},{3,7},{5,1},{7,3},{8,12},{10,14},{12... | collective-permute-start | bytes 786440 | tf_op jit(solution)/shard_map/ppermute | solution.py:29
  327.6 13.6 %collective-permute-start.78 = (f32[8,2,32,128]{3,2,0,1:T(8,128)S(1)}, f32[8,2,32,128]{3,2,0,1:T(8,128)S(1)}, u32[]{:S(2)}, u32[]{:S(2)}) collective-permute-start(f32[8,2,32,128]{3,2,0,1:T(8,128)S(1)} %collective-permute-done.77), channel_id=1, source_target_pairs={{0,1},{1,0},{2,3},{3,2},{4,5},{5,4},{6,7},{7,6},{8,9},{9,8},{10,11... | collective-permute-start | bytes 786440 | tf_op jit(solution)/shard_map/ppermute | solution.py:29
  331.4 16.7 %collective-permute-start.59 = (f32[32,2,64,128]{3,2,0,1:T(8,128)}, f32[32,2,64,128]{3,2,0,1:T(8,128)}, u32[]{:S(2)}, u32[]{:S(2)}) collective-permute-start(f32[32,2,64,128]{3,2,0,1:T(8,128)} %get-tuple-element.12), channel_id=1, source_target_pairs={{0,2},{2,0},{4,6},{6,4},{1,3},{3,1},{5,7},{7,5},{8,10},{10,8},{12,... | collective-permute-start | bytes 6291464 | tf_op jit(solution)/shard_map/ppermute | solution.py:29
  348.1 11.1 %collective-permute-start.79 = (f32[32,2,64,128]{3,2,0,1:T(8,128)}, f32[32,2,64,128]{3,2,0,1:T(8,128)}, u32[]{:S(2)}, u32[]{:S(2)}) collective-permute-start(f32[32,2,64,128]{3,2,0,1:T(8,128)} %get-tuple-element.8), channel_id=1, source_target_pairs={{0,2},{2,0},{4,6},{6,4},{1,3},{3,1},{5,7},{7,5},{8,10},{10,8},{12,... | collective-permute-start | bytes 6291464 | tf_op jit(solution)/shard_map/ppermute | solution.py:29
  (41 other events, 582.0 us)

commit v2 on v1

v2 whole, which is shorter than its diff:
```python
import functools
import math

import jax
import jax.numpy as jnp
from jax import lax
from jax.experimental import pallas as pl
from jax.experimental.pallas import tpu as pltpu
from jax.sharding import PartitionSpec as P

DIFFUSE = 0.3
PRECISION = lax.Precision.HIGH
LANES = 128
SLAB = 8
F32 = jnp.float32
VMEM = pl.BlockSpec(memory_space=pltpu.VMEM)


def cos_sin(points, waves, length):
    turns = points[:, None] * waves[None, :] % length
    angles = turns.astype(F32) * (2.0 * math.pi / length)
    return jnp.cos(angles), jnp.sin(angles)


def complex_table(cosine, sine, direction):
    turned = direction * sine
    return jnp.stack([jnp.stack([cosine, turned], axis=1), jnp.stack([-turned, cosine], axis=1)])


def contract(spec, left, right):
    return jnp.einsum(spec, left, right, precision=PRECISION)


def swap(block, axes, mask):
    count = lax.axis_size(axes)
    return lax.ppermute(block, axes, [(i, i ^ mask) for i in range(count)])


def iota(count):
    return lax.broadcasted_iota(jnp.int32, (count,), 0)


def split_table(table):
    high = lax.reduce_precision(table, 8, 7)
    return high.astype(jnp.bfloat16), (table - high).astype(jnp.bfloat16)


def split(value):
    high = value.astype(jnp.bfloat16)
    return high, (value - high.astype(F32)).astype(jnp.bfloat16)


def dot(left, right):
    return jnp.dot(left, right, preferred_element_type=F32)


def dot_turned(left, right):
    return lax.dot_general(left, right, (((1,), (1,)), ((), ())), preferred_element_type=F32)


def right_table(value, high, low):
    value_high, value_low = split(value)
    rows = value.shape[0]
    both = dot(jnp.concatenate([value_high, value_low], axis=0), high)
    return both[:rows] + both[rows:] + dot(value_high, low)


def left_table(stacked, high, value):
    value_high, value_low = split(value)
    rows = high.shape[0]
    both = dot(stacked, value_high)
    return both[:rows] + both[rows:] + dot(high, value_low)


def analyze_rows(stacked, field, near, far):
    lines, count, depth = field.shape
    waves = stacked.shape[0] // 2
    for at in range(0, lines, 2):
        pair_high, pair_low = split(field[at : at + 2].reshape(2 * count, depth))
        both = dot_turned(stacked, pair_high)
        waves_at = both[:waves] + both[waves:] + dot_turned(stacked[:waves], pair_low)
        for i in range(2):
            part = waves_at[:, i * count : (i + 1) * count]
            near[at + i] = part[: waves // 2]
            far[at + i] = part[waves // 2 :]


def analyze_kernel(table, field, near, far):
    analyze_rows(table[...], field[...], near, far)


def analyze_product_kernel(table, field, reaction, near, far):
    analyze_rows(table[...], field[...] * reaction[...], near, far)


def plane_kernel(table_y_high, table_y_low, table_x, table_x_high, near, other, *out):
    half = near.shape[0]
    waves, _, quarter, modes_y = out[0].shape
    stride = 2 * waves
    rows = half // stride

    @pl.loop(0, waves)
    def _(k):
        parts = []
        for p in range(2):
            lines = [r[pl.ds(p * waves + k, rows, stride=stride), :] for r in (near, other)]
            parts.append(jnp.concatenate(lines, axis=0))
        lines = jnp.concatenate(parts, axis=1)
        lines = right_table(lines, table_y_high[...], table_y_low[...])
        lines = jnp.concatenate([lines[:, :modes_y], lines[:, modes_y:]], axis=0)
        modes = left_table(table_x[...], table_x_high[...], lines)
        for j, ref in enumerate(out):
            for p in range(2):
                at = (2 * j + p) * quarter
                ref[k, p] = modes[at : at + quarter]


def lines_kernel(table_x, table_x_high, table_y_high, table_y_low, *refs):
    lots, by_y, by_x, cross_first, cross_second, own, send = refs
    waves, _, quarter, modes_y = cross_first.shape
    _, _, rows_x, rows_y = own.shape

    @pl.loop(0, waves)
    def _(k):
        columns = []
        for lot, cross in enumerate((cross_first, cross_second)):
            n = lot * waves + k
            pieces = [lots[n], by_y[n], by_x[n], cross[k]]
            pieces = [piece.reshape(2 * quarter, modes_y) for piece in pieces]
            columns.append(jnp.concatenate(pieces, axis=0))
        lines = left_table(table_x[...], table_x_high[...], jnp.concatenate(columns, axis=1))
        middle = lines.shape[0] // 2
        rows = []
        for lot in range(2):
            part = lines[:, lot * modes_y : (lot + 1) * modes_y]
            rows.append(jnp.concatenate([part[:middle], part[middle:]], axis=1))
        planes = right_table(jnp.concatenate(rows, axis=0), table_y_high[...], table_y_low[...])
        for lot in range(2):
            for q in range(2):
                part = planes[lot * middle : (lot + 1) * middle, q * rows_y : (q + 1) * rows_y]
                own[lot * waves + k, q] = part[:rows_x]
                send[lot * waves + k, q] = part[rows_x:]


def synthesize_rows(high, low, planes):
    lines = planes[0].shape[1]
    stacked = jnp.concatenate([high, high], axis=0)
    flat = [plane.reshape(plane.shape[0] * lines, plane.shape[2]) for plane in planes]
    for at in range(lines):
        waves = [ref[pl.ds(at, ref.shape[0] // lines, stride=lines), :] for ref in flat]
        value_high, value_low = split(jnp.concatenate(waves, axis=0).T)
        both = jnp.concatenate([value_high, value_low], axis=1)
        yield at, dot(both, stacked) + dot(value_high, low)


def rate_kernel(groups, table_high, table_low, table, reaction, before, *refs):
    planes, (rate, near, far) = refs[:groups], refs[groups:]
    for at, value in synthesize_rows(table_high[...], table_low[...], planes):
        rate[at] = value + reaction[at] * before[at]
    analyze_rows(table[...], reaction[...] * rate[...], near, far)


def total_kernel(groups, table_high, table_low, share, reaction, initial, first, second, *refs):
    planes, (total,) = refs[:groups], refs[groups:]
    for at, value in synthesize_rows(table_high[...], table_low[...], planes):
        third = value + reaction[at] * second[at]
        early = initial[at] + first[at] + share[0] * second[at]
        total[at] = early + (share[1] + share[2] * reaction[at]) * third


def last_kernel(groups, table_high, table_low, share, before, *refs):
    planes, (total,) = refs[:groups], refs[groups:]
    for at, value in synthesize_rows(table_high[...], table_low[...], planes):
        total[at] = before[at] + share[2] * value


def shards(initial, reaction):
    rows_x, rows_y, depth = initial.shape
    parts_x = lax.axis_size("gx")
    parts_y = lax.axis_size("gy")
    levels = lax.axis_size("lvl")
    full_x, full_y = rows_x * parts_x, rows_y * parts_y
    modes_x, modes_y, modes_z = full_x // 2, full_y // 2, depth // 4
    norm = 1.0 / (full_x * full_y * depth)
    level, at_x, at_y = (lax.axis_index(a) for a in ("lvl", "gx", "gy"))

    pair = at_x & 1
    extra = [("gx", 1 << k) for k in range(2, parts_x.bit_length() - 1)]
    extra += [("gy", 1 << k) for k in range(1, parts_y.bit_length() - 1)]
    place = ((at_x >> 1) & 1) * 2 + (at_y & 1)
    for axis, mask in extra:
        place = place * 2 + (lax.axis_index(axis) // mask & 1)
    blocks = parts_x // 2 * parts_y
    block_x = modes_x // blocks
    quarter = modes_x // 4
    block_z = modes_z // levels
    half_z = block_z // 2
    groups = levels // 2

    waves_x = iota(modes_x)
    waves_x = ((waves_x // block_x) ^ place) * block_x + waves_x % block_x - modes_x // 2
    waves_y = iota(modes_y) - modes_y // 2
    near_z = pair * half_z + iota(half_z)
    far_z = (1 - pair) * half_z + iota(half_z)
    points_x = jnp.concatenate([at_x * rows_x + iota(rows_x), (at_x ^ 1) * rows_x + iota(rows_x)])
    points_y = at_y * rows_y + iota(rows_y)

    cosine, sine = cos_sin(jnp.concatenate([near_z, far_z]) + level * block_z, iota(depth), depth)
    forward_z = jnp.stack([cosine.reshape(2, half_z, depth), -sine.reshape(2, half_z, depth)], axis=1)
    forward_z = forward_z.reshape(4 * half_z, depth)
    cosine_y, sine_y = cos_sin(points_y, waves_y, full_y)
    forward_y = complex_table(cosine_y, sine_y, -1.0)
    cosine_x, sine_x = cos_sin(points_x, waves_x, full_x)
    forward_x = complex_table(cosine_x, sine_x, -1.0)
    back_x = complex_table(cosine_x.T, sine_x.T, 1.0)
    back_y = complex_table(cosine_y.T, sine_y.T, 1.0)
    waves_z = []
    for group in range(groups):
        for half in (near_z, far_z):
            for lot in range(2):
                waves_z.append((level ^ (2 * group + lot)) * block_z + half)
    waves_z = jnp.concatenate(waves_z)
    cosine, sine = cos_sin(waves_z, iota(depth), depth)
    weights = jnp.where(waves_z == 0, 1.0, 2.0).astype(F32)[:, None]
    back_z = jnp.stack([cosine * weights, -sine * weights], axis=1)
    back_z = back_z.reshape(2 * modes_z, depth)

    own_z = (level * block_z + near_z)[:, None, None]
    own_x = waves_x[:block_x][None, :, None]
    own_y = waves_y[None, None, :]
    unit_x = own_x.astype(F32) / (full_x // 4)
    unit_y = own_y.astype(F32) / (full_y // 4)
    unit_z = own_z.astype(F32) / (depth // 4)
    factor_real = -DIFFUSE * (unit_x * unit_x + unit_y * unit_y + unit_z * unit_z) * norm
    factor_imag = -(0.3 * unit_x + 0.2 * unit_y + 0.25 * unit_z) * norm
    edge = (own_z == 0) & ((own_x == -(modes_x // 2)) | (own_y == -(modes_y // 2)))
    again = jnp.where(edge, 0.5, 1.0).astype(F32)[:, None] / norm
    share = [
        jnp.where(level >= k, jnp.float32(2.0**-k), jnp.float32(0.0)) for k in range(1, levels)
    ]

    tiled = rows_y % LANES == 0 and depth % LANES == 0 and rows_x % SLAB == 0
    tiled = tiled and half_z % SLAB == 0 and modes_y % LANES == 0 and quarter % SLAB == 0

    if tiled:
        steps = rows_x // SLAB
        grid_spec = pl.BlockSpec((SLAB, rows_y, depth), lambda s: (s, 0, 0))
        wave_spec = pl.BlockSpec((SLAB, 2 * half_z, rows_y), lambda s: (s, 0, 0))
        plane_spec = pl.BlockSpec((4 * half_z, SLAB, rows_y), lambda s: (0, s, 0))
        share_spec = pl.BlockSpec(memory_space=pltpu.SMEM)
        grid_shape = jax.ShapeDtypeStruct((rows_x, rows_y, depth), F32)
        wave_shape = jax.ShapeDtypeStruct((rows_x, 2 * half_z, rows_y), F32)
        waves_stacked = jnp.concatenate(split_table(forward_z), axis=0)
        back_high, back_low = split_table(back_z)
        x_table = forward_x.reshape(2, 2 * rows_x, 2, 4, quarter).transpose(3, 2, 4, 0, 1)
        x_table = x_table.reshape(8 * quarter, 4 * rows_x)
        x_high, x_low = split_table(x_table)
        x_stacked = jnp.concatenate([x_high, x_low], axis=0)
        y_high, y_low = split_table(forward_y.reshape(2 * rows_y, 2 * modes_y))
        x_back = back_x.reshape(2, 4, quarter, 2, 2 * rows_x).transpose(3, 4, 1, 0, 2)
        x_back = x_back.reshape(4 * rows_x, 8 * quarter)
        x_back_high, x_back_low = split_table(x_back)
        x_back_stacked = jnp.concatenate([x_back_high, x_back_low], axis=0)
        y_back_high, y_back_low = split_table(back_y.reshape(2 * modes_y, 2 * rows_y))
        share_array = jnp.stack(share)

        def whole(array):
            return pl.BlockSpec(array.shape, lambda s: (0,) * array.ndim)

        def by_slab(kernel, tables, blocks, out_shape, out_specs):
            specs = []
            for block in blocks:
                if block.shape == grid_shape.shape:
                    specs.append(grid_spec)
                else:
                    specs.append(plane_spec)
            table_specs = [share_spec if t is share_array else whole(t) for t in tables]
            moved = sum(math.prod(b.shape) for b in blocks) * 4
            return pl.pallas_call(
                kernel,
                grid=(steps,),
                in_specs=table_specs + specs,
                out_specs=out_specs,
                out_shape=out_shape,
                cost_estimate=pl.CostEstimate(
                    flops=12 * modes_z * rows_x * rows_y * depth,
                    bytes_accessed=moved,
                    transcendentals=0,
                ),
            )(*tables, *blocks)

        def analyze(field):
            return by_slab(
                analyze_kernel, [waves_stacked], [field], [wave_shape] * 2, [wave_spec] * 2
            )

        def analyze_product(field):
            return by_slab(
                analyze_product_kernel,
                [waves_stacked],
                [field, reaction],
                [wave_shape] * 2,
                [wave_spec] * 2,
            )

        def plane_waves(near, other):
            flat = (rows_x * 2 * half_z, rows_y)
            piece = jax.ShapeDtypeStruct((half_z, 2, quarter, modes_y), F32)
            return pl.pallas_call(
                plane_kernel,
                in_specs=[VMEM] * 6,
                out_specs=[VMEM] * 4,
                out_shape=[piece] * 4,
                cost_estimate=pl.CostEstimate(
                    flops=24 * half_z * modes_x * modes_y * 2 * (rows_x + rows_y),
                    bytes_accessed=4 * half_z * modes_x * modes_y * 4,
                    transcendentals=0,
                ),
            )(y_high, y_low, x_stacked, x_high, near.reshape(flat), other.reshape(flat))

        def plane_lines(found):
            shape = jax.ShapeDtypeStruct((2 * half_z, 2, rows_x, rows_y), F32)
            own, send = pl.pallas_call(
                lines_kernel,
                in_specs=[VMEM] * 9,
                out_specs=[VMEM] * 2,
                out_shape=[shape] * 2,
                cost_estimate=pl.CostEstimate(
                    flops=48 * half_z * modes_x * modes_y * 2 * (rows_x + rows_y),
                    bytes_accessed=8 * half_z * modes_x * modes_y * 4,
                    transcendentals=0,
                ),
            )(x_back_stacked, x_back_high, y_back_high, y_back_low, *found)
            return own, send

        def flat_planes(planes):
            return [p.reshape(4 * half_z, rows_x, rows_y) for p in planes]

        def next_rate(planes, before):
            planes = flat_planes(planes)
            return by_slab(
                functools.partial(rate_kernel, len(planes)),
                [back_high, back_low, waves_stacked],
                [reaction, before, *planes],
                [grid_shape, wave_shape, wave_shape],
                [grid_spec, wave_spec, wave_spec],
            )

        def total_before(planes, first, second):
            planes = flat_planes(planes)
            return by_slab(
                functools.partial(total_kernel, len(planes)),
                [back_high, back_low, share_array],
                [reaction, initial, first, second, *planes],
                grid_shape,
                grid_spec,
            )

        def total_last(planes, before):
            planes = flat_planes(planes)
            return by_slab(
                functools.partial(last_kernel, len(planes)),
                [back_high, back_low, share_array],
                [before, *planes],
                grid_shape,
                grid_spec,
            )

    else:

        def analyze(field):
            waves = contract("kz,xyz->xky", forward_z, field)
            return waves[:, : 2 * half_z], waves[:, 2 * half_z :]

        def analyze_product(field):
            return analyze(field * reaction)

        def plane_waves(near, other):
            lines = jnp.concatenate([near, other], axis=0)
            lines = lines.reshape(2 * rows_x, 2, half_z, rows_y)
            lines = contract("xpky,pyqm->kqxm", lines, forward_y)
            modes = contract("kpxm,pxqj->kqjm", lines, forward_x)
            return [modes[:, :, i * quarter : (i + 1) * quarter] for i in range(4)]

        def plane_lines(found):
            cross = jnp.concatenate(found[3:], axis=0)
            modes = jnp.concatenate([*found[:3], cross], axis=2)
            lines = contract("npjm,pjqx->nqxm", modes, back_x)
            lines = contract("npxm,pmqy->nqxy", lines, back_y)
            return lines[:, :, :rows_x], lines[:, :, rows_x:]

        def grid_field(planes):
            lines = jnp.concatenate(planes, axis=0).reshape(2 * modes_z, rows_x, rows_y)
            return contract("kxy,kz->xyz", lines, back_z)

        def next_rate(planes, before):
            rate = grid_field(planes) + reaction * before
            return rate, *analyze_product(rate)

        def total_before(planes, first, second):
            third = grid_field(planes) + reaction * second
            early = initial + first + share[0] * second
            return early + (share[1] + share[2] * reaction) * third

        def total_last(planes, before):
            return before + share[2] * grid_field(planes)

    def spectrum_of(near, far):
        pieces = plane_waves(near, swap(far, "gx", 1))
        total = pieces[0] + swap(pieces[1], "gy", 1) + swap(pieces[2], "gx", 2)
        total = total + swap(pieces[3], ("gx", "gy"), 2 * parts_y + 1)
        for axis, mask in extra:
            middle = total.shape[2] // 2
            total = total[:, :, :middle] + swap(total[:, :, middle:], axis, mask)
        return total

    def scaled(spectrum):
        real, imag = spectrum[:, 0], spectrum[:, 1]
        return jnp.stack(
            [
                factor_real * real - factor_imag * imag,
                factor_real * imag + factor_imag * real,
            ],
            axis=1,
        )

    def gather(piece):
        for axis, mask in reversed(extra):
            piece = jnp.concatenate([piece, swap(piece, axis, mask)], axis=2)
        lots = [jnp.concatenate([piece, swap(piece, "lvl", 1)], axis=0)]
        mask = 2
        while mask < levels:
            lots += [swap(lot, "lvl", mask) for lot in lots]
            mask *= 2
        found = []
        for lot in lots:
            by_y = swap(lot, "gy", 1)
            by_x = swap(lot, "gx", 2)
            cross_first = swap(by_y[:half_z], "gx", 2)
            cross_second = swap(by_x[half_z:], "gy", 1)
            found.append([lot, by_y, by_x, cross_first, cross_second])
        return found

    def planes_of(found):
        planes = []
        for group in found:
            own, send = plane_lines(group)
            planes += [own, swap(send, "gx", 1)]
        return planes

    first = scaled(spectrum_of(*analyze(initial)))
    first_found = gather(first)
    second = scaled(again * first + spectrum_of(*analyze_product(initial)))
    second_found = gather(second)
    rate, *waves = next_rate(planes_of(first_found), initial)
    third = scaled(again * second + spectrum_of(*waves))
    third_found = gather(third)
    rate_again, *waves = next_rate(planes_of(second_found), rate)
    fourth = scaled(again * third + spectrum_of(*waves))
    fourth_found = gather(fourth)
    total = total_before(planes_of(third_found), rate, rate_again)
    total = total_last(planes_of(fourth_found), total)
    return total[None]


def solution(mesh):
    in_specs = (P("gx", "gy", None), P("gx", "gy", None))
    out_specs = P("lvl", "gx", "gy", None)
    return jax.shard_map(shards, mesh=mesh, in_specs=in_specs, out_specs=out_specs, check_vma=False)
```

time: 392 us -> 445 us (1.14)
  Pallas kernels: 0 us -> 167 us
  matrix products: 111 us -> 0 us
  starting transfers between devices: 90.8 us -> 63.1 us
  waiting for transfers between devices: 163 us -> 183 us
  local copies, waits for them, and re-layouts: 8.38 us -> 17 us
    pallas_call x0 -> x18, Pallas kernels: none -> 167 us  [the longest x6 74.2 us: by_slab(): pl.pallas_call(kernel, grid=(steps,), in_specs=table_specs + specs, out_s...]
    dot_general x24 -> x0, matrix products: 111 us -> none  [contract(): return jnp.einsum(spec, left, right, precision=PRECISION)]
    ppermute x80 -> x64, starting transfers between devices: 90.8 us -> 63.1 us  [swap(): return lax.ppermute(block, axes, [(i, i ^ mask) for i in range(count)])]
    ppermute x80 -> x64, waiting for transfers between devices: 163 us -> 183 us  [swap(): return lax.ppermute(block, axes, [(i, i ^ mask) for i in range(count)])]
    unnamed x50 -> x75, local copies, waits for them, and re-layouts: 1.5 us -> 10.9 us
    concatenate x8 -> x7, other arithmetic: 10.6 us -> 2.24 us  [the longest x1 0.74 us: shards(): x_stacked = jnp.concatenate([x_high, x_low], axis=0)]
  transfers between devices with their start and end apart: 80 -> 64, of which waited for: 44 -> 29; matrix products, arithmetic and copies ran while one was open for 9% -> 3% of each run, Pallas kernels for 0% -> 24%
where the time goes in v2:
time: 445 us; the launch traced here: 443 us
  waiting for transfers between devices  183 us (41%)
  Pallas kernels  167 us (38%)
  starting transfers between devices  63.1 us (14%)
  local copies, waits for them, and re-layouts  17 us (4%)
  other arithmetic  12.3 us (3%)
    ppermute x64, waiting for transfers between devices, swap(): return lax.ppermute(block, axes, [(i, i ^ mask) for i in range(count)])  183 us
    pallas_call x6, Pallas kernels, by_slab(): pl.pallas_call(kernel, grid=(steps,), in_specs=table_specs + specs, out_s...  74.2 us
    pallas_call x8, Pallas kernels, plane_lines(): pl.pallas_call(lines_kernel, in_specs=[VMEM] * 9, out_specs=[VMEM] * 2, o...  65.7 us
    ppermute x64, starting transfers between devices, swap(): return lax.ppermute(block, axes, [(i, i ^ mask) for i in range(count)])  63.1 us
    pallas_call x4, Pallas kernels, plane_waves(): pl.pallas_call(plane_kernel, in_specs=[VMEM] * 6, out_specs=[VMEM] * 4, o...  27.2 us
    unnamed x75, local copies, waits for them, and re-layouts  10.9 us
  transfers between devices with their start and end apart: 64, of which 29 were waited for; matrix products, arithmetic and copies ran while one was open for 3% of the time, Pallas kernels for 24%

profile of v2, /device:TPU:0, one launch (start us, length us, event | category | flops | bytes accessed | tf_op | source)
XLA Modules:
  0.0 443.1 jit_solution(8638934271105968641)
XLA Ops:
  1.0 9.8 %shard_map.33 = (f32[64,16,128]{2,1,0:T(8,128)}, f32[64,16,128]{2,1,0:T(8,128)}) custom-call(bf16[64,256]{1,0:T(8,128)(2,1)} %pad_maximum_fusion.14.table, f32[64,128,256]{2,1,0:T(8,128)} %initial.1, f32[64,128,256]{2,1,0:T(8,128)} %reaction.7), custom_call_target="tpu_custom_call" | custom-call | flops 1610612736 | bytes 16777216 | tf_op jit(solution)/shard_map/pallas_call | solution.py:279
  11.3 8.2 %shard_map.28 = (f32[64,16,128]{2,1,0:T(8,128)}, f32[64,16,128]{2,1,0:T(8,128)}) custom-call(bf16[64,256]{1,0:T(8,128)(2,1)} %pad_maximum_fusion.14.table, f32[64,128,256]{2,1,0:T(8,128)} %initial.1), custom_call_target="tpu_custom_call" | custom-call | flops 1610612736 | bytes 8388608 | tf_op jit(solution)/shard_map/pallas_call | solution.py:279
  23.8 6.8 %shard_map.29 = (f32[8,2,32,128]{3,2,1,0:T(8,128)}, f32[8,2,32,128]{3,2,1,0:T(8,128)}, f32[8,2,32,128]{3,2,1,0:T(8,128)}, f32[8,2,32,128]{3,2,1,0:T(8,128)}) custom-call(bf16[256,256]{1,0:T(8,128)(2,1)} %get-tuple-element.108.table_y_high, bf16[256,256]{1,0:T(8,128)(2,1)} %get-tuple-element.107.table_y_low, bf16[512,256]{1,0:T(8,128)(2,1)} %pad_maximum_fusion.7.table_x, ...), custom_call_target="tpu_custom_call" | custom-call | flops 1207959552 | bytes 2097152 | tf_op jit(solution)/shard_map/pallas_call | solution.py:309
  30.7 3.9 collective-permute-start.3
  36.0 6.8 %shard_map.34 = (f32[8,2,32,128]{3,2,1,0:T(8,128)}, f32[8,2,32,128]{3,2,1,0:T(8,128)}, f32[8,2,32,128]{3,2,1,0:T(8,128)}, f32[8,2,32,128]{3,2,1,0:T(8,128)}) custom-call(bf16[256,256]{1,0:T(8,128)(2,1)} %get-tuple-element.108.table_y_high, bf16[256,256]{1,0:T(8,128)(2,1)} %get-tuple-element.107.table_y_low, bf16[512,256]{1,0:T(8,128)(2,1)} %pad_maximum_fusion.7.table_x, ...), custom_call_target="tpu_custom_call" | custom-call | flops 1207959552 | bytes 2097152 | tf_op jit(solution)/shard_map/pallas_call | solution.py:309
  42.8 2.9 collective-permute-start.19
  49.3 4.0 collective-permute-done.19
  53.3 4.9 %collective-permute-done.18 = f32[8,2,32,128]{3,2,1,0:T(8,128)S(1)} collective-permute-done((f32[8,2,32,128]{3,2,1,0:T(8,128)}, f32[8,2,32,128]{3,2,1,0:T(8,128)S(1)}, u32[]{:S(2)}, u32[]{:S(2)}) %collective-permute-start.18) | collective-permute-done | bytes 262176 | tf_op jit(solution)/shard_map/ppermute | solution.py:36
  59.6 1.6 collective-permute-start.4
  61.2 6.3 %collective-permute-done.4 = f32[8,2,32,128]{3,2,1,0:T(8,128)S(1)} collective-permute-done((f32[8,2,32,128]{3,2,1,0:T(8,128)S(1)}, f32[8,2,32,128]{3,2,1,0:T(8,128)S(1)}, u32[]{:S(2)}, u32[]{:S(2)}) %collective-permute-start.4) | collective-permute-done | bytes 262176 | tf_op jit(solution)/shard_map/ppermute | solution.py:36
  67.6 2.8 collective-permute-start.10
  70.4 1.5 collective-permute-start.5
  73.0 19.8 %collective-permute-done.10.refs_0_ = f32[16,2,32,128]{3,2,1,0:T(8,128)} collective-permute-done((f32[16,2,32,128]{3,2,1,0:T(8,128)S(1)}, f32[16,2,32,128]{3,2,1,0:T(8,128)}, u32[]{:S(2)}, u32[]{:S(2)}) %collective-permute-start.10) | collective-permute-done | bytes 524320 | tf_op jit(solution)/shard_map/ppermute | solution.py:36
  92.8 1.5 collective-permute-start.11
  94.6 1.9 collective-permute-start.7
  99.5 8.4 %collective-permute-done.11.refs_1_ = f32[16,2,32,128]{3,2,1,0:T(8,128)} collective-permute-done((f32[16,2,32,128]{3,2,1,0:T(8,128)}, f32[16,2,32,128]{3,2,1,0:T(8,128)}, u32[]{:S(2)}, u32[]{:S(2)}) %collective-permute-start.11) | collective-permute-done | bytes 524320 | tf_op jit(solution)/shard_map/ppermute | solution.py:36
  108.9 1.8 collective-permute-start.13
  111.7 3.2 collective-permute-done.7.refs_3_
  115.7 8.2 %shard_map.30 = (f32[16,2,64,128]{3,2,1,0:T(8,128)}, f32[16,2,64,128]{3,2,1,0:T(8,128)}) custom-call(bf16[512,256]{1,0:T(8,128)(2,1)} %pad_maximum_fusion.4.table_x, bf16[256,256]{1,0:T(8,128)(2,1)} %copy-done.11, bf16[256,256]{1,0:T(8,128)(2,1)} %get-tuple-element.110.table_y_high, bf16[256,256]{1,0:T(8,128)(2,1)} %get-tuple-element.109.table_y_low, ...), custom_call_target="tpu_custom_call" | custom-call | flops 2415919104 | bytes 4194304 | tf_op jit(solution)/shard_map/pallas_call | solution.py:323
  124.6 8.2 %shard_map.31 = (f32[16,2,64,128]{3,2,1,0:T(8,128)}, f32[16,2,64,128]{3,2,1,0:T(8,128)}) custom-call(bf16[512,256]{1,0:T(8,128)(2,1)} %pad_maximum_fusion.4.table_x, bf16[256,256]{1,0:T(8,128)(2,1)} %copy-done.11, bf16[256,256]{1,0:T(8,128)(2,1)} %get-tuple-element.110.table_y_high, bf16[256,256]{1,0:T(8,128)(2,1)} %get-tuple-element.109.table_y_low, ...), custom_call_target="tpu_custom_call" | custom-call | flops 2415919104 | bytes 4194304 | tf_op jit(solution)/shard_map/pallas_call | solution.py:323
  136.8 13.7 %shard_map.32 = (f32[64,128,256]{2,1,0:T(8,128)}, f32[64,16,128]{2,1,0:T(8,128)}, f32[64,16,128]{2,1,0:T(8,128)}) custom-call(bf16[128,256]{1,0:T(8,128)(2,1)} %get-tuple-element.114.table_high, bf16[128,256]{1,0:T(8,128)(2,1)} %get-tuple-element.113.table_low, bf16[64,256]{1,0:T(8,128)(2,1)} %pad_maximum_fusion.14.table, f32[64,128,256]{2,1,0:T(8,128)} %reaction.7, ...), custom_call_target="tpu_custom_call" | custom-call | flops 1610612736 | bytes 20971520 | tf_op jit(solution)/shard_map/pallas_call | solution.py:279
  151.0 1.7 collective-permute-done.32
  153.5 6.8 %shard_map.38 = (f32[8,2,32,128]{3,2,1,0:T(8,128)}, f32[8,2,32,128]{3,2,1,0:T(8,128)}, f32[8,2,32,128]{3,2,1,0:T(8,128)}, f32[8,2,32,128]{3,2,1,0:T(8,128)}) custom-call(bf16[256,256]{1,0:T(8,128)(2,1)} %get-tuple-element.108.table_y_high, bf16[256,256]{1,0:T(8,128)(2,1)} %get-tuple-element.107.table_y_low, bf16[512,256]{1,0:T(8,128)(2,1)} %pad_maximum_fusion.7.table_x, ...), custom_call_target="tpu_custom_call" | custom-call | flops 1207959552 | bytes 2097152 | tf_op jit(solution)/shard_map/pallas_call | solution.py:309
  160.3 1.6 collective-permute-start.35
  162.3 1.5 collective-permute-start.33
  163.9 6.7 %collective-permute-done.35 = f32[8,2,32,128]{3,2,1,0:T(8,128)S(1)} collective-permute-done((f32[8,2,32,128]{3,2,1,0:T(8,128)}, f32[8,2,32,128]{3,2,1,0:T(8,128)S(1)}, u32[]{:S(2)}, u32[]{:S(2)}) %collective-permute-start.35) | collective-permute-done | bytes 262176 | tf_op jit(solution)/shard_map/ppermute | solution.py:36
  170.7 5.0 %collective-permute-done.34 = f32[8,2,32,128]{3,2,1,0:T(8,128)S(1)} collective-permute-done((f32[8,2,32,128]{3,2,1,0:T(8,128)}, f32[8,2,32,128]{3,2,1,0:T(8,128)S(1)}, u32[]{:S(2)}, u32[]{:S(2)}) %collective-permute-start.34) | collective-permute-done | bytes 262176 | tf_op jit(solution)/shard_map/ppermute | solution.py:36
  177.4 7.7 %collective-permute-done.20 = f32[8,2,32,128]{3,2,1,0:T(8,128)S(1)} collective-permute-done((f32[8,2,32,128]{3,2,1,0:T(8,128)S(1)}, f32[8,2,32,128]{3,2,1,0:T(8,128)S(1)}, u32[]{:S(2)}, u32[]{:S(2)}) %collective-permute-start.20) | collective-permute-done | bytes 262176 | tf_op jit(solution)/shard_map/ppermute | solution.py:36
  185.1 2.4 collective-permute-start.26
  188.0 1.7 collective-permute-start.22
  189.7 20.6 %collective-permute-done.26.refs_0_ = f32[16,2,32,128]{3,2,1,0:T(8,128)S(1)} collective-permute-done((f32[16,2,32,128]{3,2,1,0:T(8,128)S(1)}, f32[16,2,32,128]{3,2,1,0:T(8,128)S(1)}, u32[]{:S(2)}, u32[]{:S(2)}) %collective-permute-start.26) | collective-permute-done | bytes 524320 | tf_op jit(solution)/shard_map/ppermute | solution.py:36
  210.6 1.9 collective-permute-start.28
  214.6 10.5 %collective-permute-done.27.refs_1_ = f32[16,2,32,128]{3,2,1,0:T(8,128)S(1)} collective-permute-done((f32[16,2,32,128]{3,2,1,0:T(8,128)S(1)}, f32[16,2,32,128]{3,2,1,0:T(8,128)S(1)}, u32[]{:S(2)}, u32[]{:S(2)}) %collective-permute-start.27) | collective-permute-done | bytes 524320 | tf_op jit(solution)/shard_map/ppermute | solution.py:36
  225.4 2.1 collective-permute-start.30
  227.5 3.5 collective-permute-done.23.refs_3_
  231.7 8.2 %shard_map.35 = (f32[16,2,64,128]{3,2,1,0:T(8,128)}, f32[16,2,64,128]{3,2,1,0:T(8,128)}) custom-call(bf16[512,256]{1,0:T(8,128)(2,1)} %pad_maximum_fusion.4.table_x, bf16[256,256]{1,0:T(8,128)(2,1)} %copy-done.11, bf16[256,256]{1,0:T(8,128)(2,1)} %get-tuple-element.110.table_y_high, bf16[256,256]{1,0:T(8,128)(2,1)} %get-tuple-element.109.table_y_low, ...), custom_call_target="tpu_custom_call" | custom-call | flops 2415919104 | bytes 4194304 | tf_op jit(solution)/shard_map/pallas_call | solution.py:323
  240.6 8.2 %shard_map.36 = (f32[16,2,64,128]{3,2,1,0:T(8,128)}, f32[16,2,64,128]{3,2,1,0:T(8,128)}) custom-call(bf16[512,256]{1,0:T(8,128)(2,1)} %pad_maximum_fusion.4.table_x, bf16[256,256]{1,0:T(8,128)(2,1)} %copy-done.11, bf16[256,256]{1,0:T(8,128)(2,1)} %get-tuple-element.110.table_y_high, bf16[256,256]{1,0:T(8,128)(2,1)} %get-tuple-element.109.table_y_low, ...), custom_call_target="tpu_custom_call" | custom-call | flops 2415919104 | bytes 4194304 | tf_op jit(solution)/shard_map/pallas_call | solution.py:323
  249.3 2.5 collective-permute-done.31
  252.8 13.8 %shard_map.37 = (f32[64,128,256]{2,1,0:T(8,128)}, f32[64,16,128]{2,1,0:T(8,128)}, f32[64,16,128]{2,1,0:T(8,128)}) custom-call(bf16[128,256]{1,0:T(8,128)(2,1)} %get-tuple-element.114.table_high, bf16[128,256]{1,0:T(8,128)(2,1)} %get-tuple-element.113.table_low, bf16[64,256]{1,0:T(8,128)(2,1)} %pad_maximum_fusion.14.table, f32[64,128,256]{2,1,0:T(8,128)} %reaction.7, ...), custom_call_target="tpu_custom_call" | custom-call | flops 1610612736 | bytes 20971520 | tf_op jit(solution)/shard_map/pallas_call | solution.py:279
  267.0 1.7 collective-permute-done.48
  269.6 6.8 %shard_map.42 = (f32[8,2,32,128]{3,2,1,0:T(8,128)}, f32[8,2,32,128]{3,2,1,0:T(8,128)}, f32[8,2,32,128]{3,2,1,0:T(8,128)}, f32[8,2,32,128]{3,2,1,0:T(8,128)}) custom-call(bf16[256,256]{1,0:T(8,128)(2,1)} %get-tuple-element.108.table_y_high, bf16[256,256]{1,0:T(8,128)(2,1)} %get-tuple-element.107.table_y_low, bf16[512,256]{1,0:T(8,128)(2,1)} %pad_maximum_fusion.7.table_x, ...), custom_call_target="tpu_custom_call" | custom-call | flops 1207959552 | bytes 2097152 | tf_op jit(solution)/shard_map/pallas_call | solution.py:309
  277.7 1.8 collective-permute-start.50
  280.0 6.7 %collective-permute-done.51 = f32[8,2,32,128]{3,2,1,0:T(8,128)S(1)} collective-permute-done((f32[8,2,32,128]{3,2,1,0:T(8,128)}, f32[8,2,32,128]{3,2,1,0:T(8,128)S(1)}, u32[]{:S(2)}, u32[]{:S(2)}) %collective-permute-start.51) | collective-permute-done | bytes 262176 | tf_op jit(solution)/shard_map/ppermute | solution.py:36
  286.7 5.0 %collective-permute-done.50 = f32[8,2,32,128]{3,2,1,0:T(8,128)S(1)} collective-permute-done((f32[8,2,32,128]{3,2,1,0:T(8,128)}, f32[8,2,32,128]{3,2,1,0:T(8,128)S(1)}, u32[]{:S(2)}, u32[]{:S(2)}) %collective-permute-start.50) | collective-permute-done | bytes 262176 | tf_op jit(solution)/shard_map/ppermute | solution.py:36
  294.2 1.4 collective-permute-start.52
  295.6 6.9 %collective-permute-done.36 = f32[8,2,32,128]{3,2,1,0:T(8,128)S(1)} collective-permute-done((f32[8,2,32,128]{3,2,1,0:T(8,128)S(1)}, f32[8,2,32,128]{3,2,1,0:T(8,128)S(1)}, u32[]{:S(2)}, u32[]{:S(2)}) %collective-permute-start.36) | collective-permute-done | bytes 262176 | tf_op jit(solution)/shard_map/ppermute | solution.py:36
  304.5 2.0 collective-permute-start.42
  306.5 3.0 collective-permute-done.52
  309.6 2.0 collective-permute-start.53
  311.6 5.8 %collective-permute-done.37.refs_1_ = f32[16,2,32,128]{3,2,1,0:T(8,128)S(1)} collective-permute-done((f32[16,2,32,128]{3,2,1,0:T(8,128)S(1)}, f32[16,2,32,128]{3,2,1,0:T(8,128)S(1)}, u32[]{:S(2)}, u32[]{:S(2)}) %collective-permute-start.37) | collective-permute-done | bytes 524320 | tf_op jit(solution)/shard_map/ppermute | solution.py:36
  318.6 23.3 %collective-permute-done.42.refs_0_ = f32[16,2,32,128]{3,2,1,0:T(8,128)S(1)} collective-permute-done((f32[16,2,32,128]{3,2,1,0:T(8,128)S(1)}, f32[16,2,32,128]{3,2,1,0:T(8,128)S(1)}, u32[]{:S(2)}, u32[]{:S(2)}) %collective-permute-start.42) | collective-permute-done | bytes 524320 | tf_op jit(solution)/shard_map/ppermute | solution.py:36
  341.9 1.9 collective-permute-start.43
  344.0 1.9 collective-permute-start.39
  345.9 4.8 %collective-permute-done.58.refs_0_ = f32[16,2,32,128]{3,2,1,0:T(8,128)} collective-permute-done((f32[16,2,32,128]{3,2,1,0:T(8,128)S(1)}, f32[16,2,32,128]{3,2,1,0:T(8,128)}, u32[]{:S(2)}, u32[]{:S(2)}) %collective-permute-start.58) | collective-permute-done | bytes 524320 | tf_op jit(solution)/shard_map/ppermute | solution.py:36
  350.7 1.7 collective-permute-start.59
  352.6 10.2 %collective-permute-done.39.refs_3_ = f32[8,2,32,128]{3,2,1,0:T(8,128)S(1)} collective-permute-done((f32[8,2,32,128]{3,2,1,0:T(8,128)S(1)}, f32[8,2,32,128]{3,2,1,0:T(8,128)S(1)}, u32[]{:S(2)}, u32[]{:S(2)}) %collective-permute-start.39) | collective-permute-done | bytes 262176 | tf_op jit(solution)/shard_map/ppermute | solution.py:36
  365.4 6.6 %collective-permute-done.40.refs_4_ = f32[8,2,32,128]{3,2,1,0:T(8,128)S(1)} collective-permute-done((f32[8,2,32,128]{3,2,1,0:T(8,128)S(1)}, f32[8,2,32,128]{3,2,1,0:T(8,128)S(1)}, u32[]{:S(2)}, u32[]{:S(2)}) %collective-permute-start.40) | collective-permute-done | bytes 262176 | tf_op jit(solution)/shard_map/ppermute | solution.py:36
  373.8 8.2 %shard_map.39 = (f32[16,2,64,128]{3,2,1,0:T(8,128)}, f32[16,2,64,128]{3,2,1,0:T(8,128)}) custom-call(bf16[512,256]{1,0:T(8,128)(2,1)} %pad_maximum_fusion.4.table_x, bf16[256,256]{1,0:T(8,128)(2,1)} %copy-done.11, bf16[256,256]{1,0:T(8,128)(2,1)} %get-tuple-element.110.table_y_high, bf16[256,256]{1,0:T(8,128)(2,1)} %get-tuple-element.109.table_y_low, ...), custom_call_target="tpu_custom_call" | custom-call | flops 2415919104 | bytes 4194304 | tf_op jit(solution)/shard_map/pallas_call | solution.py:323
  382.1 1.7 slice.123
  386.2 8.2 %shard_map.43 = (f32[16,2,64,128]{3,2,1,0:T(8,128)}, f32[16,2,64,128]{3,2,1,0:T(8,128)}) custom-call(bf16[512,256]{1,0:T(8,128)(2,1)} %pad_maximum_fusion.4.table_x, bf16[256,256]{1,0:T(8,128)(2,1)} %copy-done.11, bf16[256,256]{1,0:T(8,128)(2,1)} %get-tuple-element.110.table_y_high, bf16[256,256]{1,0:T(8,128)(2,1)} %get-tuple-element.109.table_y_low, ...), custom_call_target="tpu_custom_call" | custom-call | flops 2415919104 | bytes 4194304 | tf_op jit(solution)/shard_map/pallas_call | solution.py:323
  394.5 8.2 %shard_map.40 = (f32[16,2,64,128]{3,2,1,0:T(8,128)}, f32[16,2,64,128]{3,2,1,0:T(8,128)}) custom-call(bf16[512,256]{1,0:T(8,128)(2,1)} %pad_maximum_fusion.4.table_x, bf16[256,256]{1,0:T(8,128)(2,1)} %copy-done.11, bf16[256,256]{1,0:T(8,128)(2,1)} %get-tuple-element.110.table_y_high, bf16[256,256]{1,0:T(8,128)(2,1)} %get-tuple-element.109.table_y_low, ...), custom_call_target="tpu_custom_call" | custom-call | flops 2415919104 | bytes 4194304 | tf_op jit(solution)/shard_map/pallas_call | solution.py:323
  403.3 8.3 %shard_map.44 = (f32[16,2,64,128]{3,2,1,0:T(8,128)}, f32[16,2,64,128]{3,2,1,0:T(8,128)}) custom-call(bf16[512,256]{1,0:T(8,128)(2,1)} %pad_maximum_fusion.4.table_x, bf16[256,256]{1,0:T(8,128)(2,1)} %copy-done.11, bf16[256,256]{1,0:T(8,128)(2,1)} %get-tuple-element.110.table_y_high, bf16[256,256]{1,0:T(8,128)(2,1)} %get-tuple-element.109.table_y_low, ...), custom_call_target="tpu_custom_call" | custom-call | flops 2415919104 | bytes 4194304 | tf_op jit(solution)/shard_map/pallas_call | solution.py:323
  413.5 17.2 %shard_map.41.before = f32[64,128,256]{2,1,0:T(8,128)} custom-call(bf16[128,256]{1,0:T(8,128)(2,1)} %get-tuple-element.114.table_high, bf16[128,256]{1,0:T(8,128)(2,1)} %get-tuple-element.113.table_low, f32[3]{0:T(128)} %pad_maximum_fusion.15.share, f32[64,128,256]{2,1,0:T(8,128)} %reaction.7, f32[64,128,256]{2,1,0:T(8,128)} %initial.1, ...), custom_call_target="tpu_custom_call" | custom-call | flops 1610612736 | bytes 37748736 | tf_op jit(solution)/shard_map/pallas_call | solution.py:279
  431.6 11.4 %shard_map.45 = f32[64,128,256]{2,1,0:T(8,128)} custom-call(bf16[128,256]{1,0:T(8,128)(2,1)} %get-tuple-element.114.table_high, bf16[128,256]{1,0:T(8,128)(2,1)} %get-tuple-element.113.table_low, f32[3]{0:T(128)} %pad_maximum_fusion.15.share, f32[64,128,256]{2,1,0:T(8,128)} %shard_map.41.before, f32[32,64,128]{2,1,0:T(8,128)} %bitcast.67, ...), custom_call_target="tpu_custom_call" | custom-call | flops 1610612736 | bytes 12582912 | tf_op jit(solution)/shard_map/pallas_call | solution.py:279
  (240 shorter events, 52.7 us)
Async XLA Ops:
  10.8 24.4 %collective-permute-start.16 = (f32[64,16,128]{2,1,0:T(8,128)}, f32[64,16,128]{2,1,0:T(8,128)S(1)}, u32[]{:S(2)}, u32[]{:S(2)}) collective-permute-start(f32[64,16,128]{2,1,0:T(8,128)} %get-tuple-element.59), channel_id=1, source_target_pairs={{0,2},{2,0},{4,6},{6,4},{1,3},{3,1},{5,7},{7,5},{8,10},{10,8},{12,... | collective-permute-start | bytes 1572872 | tf_op jit(solution)/shard_map/ppermute | solution.py:36
  19.5 3.5 collective-permute-start
  30.7 15.5 %collective-permute-start.3 = (f32[8,2,32,128]{3,2,1,0:T(8,128)}, f32[8,2,32,128]{3,2,1,0:T(8,128)S(1)}, u32[]{:S(2)}, u32[]{:S(2)}) collective-permute-start(f32[8,2,32,128]{3,2,1,0:T(8,128)} %get-tuple-element.52), channel_id=1, source_target_pairs={{0,5},{1,4},{2,7},{3,6},{4,1},{5,0},{6,3},{7,2},{8,13},{9,12},{10,... | collective-permute-start | bytes 786440 | tf_op jit(solution)/shard_map/ppermute | solution.py:36
  34.6 13.1 %collective-permute-start.2 = (f32[8,2,32,128]{3,2,1,0:T(8,128)}, f32[8,2,32,128]{3,2,1,0:T(8,128)S(1)}, u32[]{:S(2)}, u32[]{:S(2)}) collective-permute-start(f32[8,2,32,128]{3,2,1,0:T(8,128)} %get-tuple-element.51), channel_id=1, source_target_pairs={{0,4},{2,6},{4,0},{6,2},{1,5},{3,7},{5,1},{7,3},{8,12},{10,14},{12... | collective-permute-start | bytes 786440 | tf_op jit(solution)/shard_map/ppermute | solution.py:36
  35.1 13.1 %collective-permute-start.1 = (f32[8,2,32,128]{3,2,1,0:T(8,128)}, f32[8,2,32,128]{3,2,1,0:T(8,128)S(1)}, u32[]{:S(2)}, u32[]{:S(2)}) collective-permute-start(f32[8,2,32,128]{3,2,1,0:T(8,128)} %get-tuple-element.50), channel_id=1, source_target_pairs={{0,1},{1,0},{2,3},{3,2},{4,5},{5,4},{6,7},{7,6},{8,9},{9,8},{10,11... | collective-permute-start | bytes 786440 | tf_op jit(solution)/shard_map/ppermute | solution.py:36
  42.8 10.5 %collective-permute-start.19 = (f32[8,2,32,128]{3,2,1,0:T(8,128)}, f32[8,2,32,128]{3,2,1,0:T(8,128)S(1)}, u32[]{:S(2)}, u32[]{:S(2)}) collective-permute-start(f32[8,2,32,128]{3,2,1,0:T(8,128)} %get-tuple-element.63), channel_id=1, source_target_pairs={{0,5},{1,4},{2,7},{3,6},{4,1},{5,0},{6,3},{7,2},{8,13},{9,12},{10,... | collective-permute-start | bytes 786440 | tf_op jit(solution)/shard_map/ppermute | solution.py:36
  45.7 12.4 %collective-permute-start.18 = (f32[8,2,32,128]{3,2,1,0:T(8,128)}, f32[8,2,32,128]{3,2,1,0:T(8,128)S(1)}, u32[]{:S(2)}, u32[]{:S(2)}) collective-permute-start(f32[8,2,32,128]{3,2,1,0:T(8,128)} %get-tuple-element.62), channel_id=1, source_target_pairs={{0,4},{2,6},{4,0},{6,2},{1,5},{3,7},{5,1},{7,3},{8,12},{10,14},{12... | collective-permute-start | bytes 786440 | tf_op jit(solution)/shard_map/ppermute | solution.py:36
  46.2 12.3 %collective-permute-start.17 = (f32[8,2,32,128]{3,2,1,0:T(8,128)}, f32[8,2,32,128]{3,2,1,0:T(8,128)S(1)}, u32[]{:S(2)}, u32[]{:S(2)}) collective-permute-start(f32[8,2,32,128]{3,2,1,0:T(8,128)} %get-tuple-element.61), channel_id=1, source_target_pairs={{0,1},{1,0},{2,3},{3,2},{4,5},{5,4},{6,7},{7,6},{8,9},{9,8},{10,11... | collective-permute-start | bytes 786440 | tf_op jit(solution)/shard_map/ppermute | solution.py:36
  59.6 7.9 %collective-permute-start.4 = (f32[8,2,32,128]{3,2,1,0:T(8,128)S(1)}, f32[8,2,32,128]{3,2,1,0:T(8,128)S(1)}, u32[]{:S(2)}, u32[]{:S(2)}) collective-permute-start(f32[8,2,32,128]{3,2,1,0:T(8,128)S(1)} %get-tuple-element.104), channel_id=1, source_target_pairs={{0,8},{8,0},{16,24},{24,16},{1,9},{9,1},{17,25},{25,17},{2,10},{10... | collective-permute-start | bytes 786440 | tf_op jit(solution)/shard_map/ppermute | solution.py:36
  67.6 25.2 %collective-permute-start.10 = (f32[16,2,32,128]{3,2,1,0:T(8,128)S(1)}, f32[16,2,32,128]{3,2,1,0:T(8,128)}, u32[]{:S(2)}, u32[]{:S(2)}) collective-permute-start(f32[16,2,32,128]{3,2,1,0:T(8,128)S(1)} %pad_maximum_fusion.refs_0_), channel_id=1, source_target_pairs={{0,16},{8,24},{16,0},{24,8},{1,17},{9,25},{17,1},{25,9},{2,18},{10... | collective-permute-start | bytes 1572872 | tf_op jit(solution)/shard_map/ppermute | solution.py:36
  70.4 24.2 %collective-permute-start.5 = (f32[16,2,32,128]{3,2,1,0:T(8,128)S(1)}, f32[16,2,32,128]{3,2,1,0:T(8,128)S(1)}, u32[]{:S(2)}, u32[]{:S(2)}) collective-permute-start(f32[16,2,32,128]{3,2,1,0:T(8,128)S(1)} %pad_maximum_fusion.refs_0_), channel_id=1, source_target_pairs={{0,1},{1,0},{2,3},{3,2},{4,5},{5,4},{6,7},{7,6},{8,9},{9,8},{10,11... | collective-permute-start | bytes 1572872 | tf_op jit(solution)/shard_map/ppermute | solution.py:36
  71.9 24.6 %collective-permute-start.6 = (f32[16,2,32,128]{3,2,1,0:T(8,128)S(1)}, f32[16,2,32,128]{3,2,1,0:T(8,128)}, u32[]{:S(2)}, u32[]{:S(2)}) collective-permute-start(f32[16,2,32,128]{3,2,1,0:T(8,128)S(1)} %pad_maximum_fusion.refs_0_), channel_id=1, source_target_pairs={{0,4},{2,6},{4,0},{6,2},{1,5},{3,7},{5,1},{7,3},{8,12},{10,14},{12... | collective-permute-start | bytes 1572872 | tf_op jit(solution)/shard_map/ppermute | solution.py:36
  92.8 15.1 %collective-permute-start.11 = (f32[16,2,32,128]{3,2,1,0:T(8,128)}, f32[16,2,32,128]{3,2,1,0:T(8,128)}, u32[]{:S(2)}, u32[]{:S(2)}) collective-permute-start(f32[16,2,32,128]{3,2,1,0:T(8,128)} %collective-permute-done.10.refs_0_), channel_id=1, source_target_pairs={{0,1},{1,0},{2,3},{3,2},{4,5},{5,4},{6,7},{7,6},{8,9},{9,8},{10,11... | collective-permute-start | bytes 1572872 | tf_op jit(solution)/shard_map/ppermute | solution.py:36
  94.3 16.3 %collective-permute-start.12 = (f32[16,2,32,128]{3,2,1,0:T(8,128)}, f32[16,2,32,128]{3,2,1,0:T(8,128)}, u32[]{:S(2)}, u32[]{:S(2)}) collective-permute-start(f32[16,2,32,128]{3,2,1,0:T(8,128)} %collective-permute-done.10.refs_0_), channel_id=1, source_target_pairs={{0,4},{2,6},{4,0},{6,2},{1,5},{3,7},{5,1},{7,3},{8,12},{10,14},{12... | collective-permute-start | bytes 1572872 | tf_op jit(solution)/shard_map/ppermute | solution.py:36
  94.6 20.3 %collective-permute-start.7 = (f32[8,2,32,128]{3,2,1,0:T(8,128)S(1)}, f32[8,2,32,128]{3,2,1,0:T(8,128)S(1)}, u32[]{:S(2)}, u32[]{:S(2)}) collective-permute-start(f32[8,2,32,128]{3,2,1,0:T(8,128)S(1)} %slice.102), channel_id=1, source_target_pairs={{0,4},{2,6},{4,0},{6,2},{1,5},{3,7},{5,1},{7,3},{8,12},{10,14},{12... | collective-permute-start | bytes 786440 | tf_op jit(solution)/shard_map/ppermute | solution.py:36
  97.5 17.5 %collective-permute-start.8 = (f32[8,2,32,128]{3,2,1,0:T(8,128)S(1)}, f32[8,2,32,128]{3,2,1,0:T(8,128)}, u32[]{:S(2)}, u32[]{:S(2)}) collective-permute-start(f32[8,2,32,128]{3,2,1,0:T(8,128)S(1)} %slice.103), channel_id=1, source_target_pairs={{0,1},{1,0},{2,3},{3,2},{4,5},{5,4},{6,7},{7,6},{8,9},{9,8},{10,11... | collective-permute-start | bytes 786440 | tf_op jit(solution)/shard_map/ppermute | solution.py:36
  108.9 15.0 %collective-permute-start.13 = (f32[8,2,32,128]{3,2,1,0:T(8,128)S(1)}, f32[8,2,32,128]{3,2,1,0:T(8,128)}, u32[]{:S(2)}, u32[]{:S(2)}) collective-permute-start(f32[8,2,32,128]{3,2,1,0:T(8,128)S(1)} %slice.104), channel_id=1, source_target_pairs={{0,4},{2,6},{4,0},{6,2},{1,5},{3,7},{5,1},{7,3},{8,12},{10,14},{12... | collective-permute-start | bytes 786440 | tf_op jit(solution)/shard_map/ppermute | solution.py:36
  111.6 12.2 %collective-permute-start.14 = (f32[8,2,32,128]{3,2,1,0:T(8,128)S(1)}, f32[8,2,32,128]{3,2,1,0:T(8,128)S(1)}, u32[]{:S(2)}, u32[]{:S(2)}) collective-permute-start(f32[8,2,32,128]{3,2,1,0:T(8,128)S(1)} %slice.105), channel_id=1, source_target_pairs={{0,1},{1,0},{2,3},{3,2},{4,5},{5,4},{6,7},{7,6},{8,9},{9,8},{10,11... | collective-permute-start | bytes 786440 | tf_op jit(solution)/shard_map/ppermute | solution.py:36
  123.8 10.8 %collective-permute-start.9 = (f32[16,2,64,128]{3,2,1,0:T(8,128)}, f32[16,2,64,128]{3,2,1,0:T(8,128)S(1)}, u32[]{:S(2)}, u32[]{:S(2)}) collective-permute-start(f32[16,2,64,128]{3,2,1,0:T(8,128)} %get-tuple-element.54), channel_id=1, source_target_pairs={{0,2},{2,0},{4,6},{6,4},{1,3},{3,1},{5,7},{7,5},{8,10},{10,8},{12,... | collective-permute-start | bytes 3145736 | tf_op jit(solution)/shard_map/ppermute | solution.py:36
  132.8 3.0 collective-permute-start.15
  150.5 2.2 collective-permute-start.32
  160.3 10.3 %collective-permute-start.35 = (f32[8,2,32,128]{3,2,1,0:T(8,128)}, f32[8,2,32,128]{3,2,1,0:T(8,128)S(1)}, u32[]{:S(2)}, u32[]{:S(2)}) collective-permute-start(f32[8,2,32,128]{3,2,1,0:T(8,128)} %get-tuple-element.74), channel_id=1, source_target_pairs={{0,5},{1,4},{2,7},{3,6},{4,1},{5,0},{6,3},{7,2},{8,13},{9,12},{10,... | collective-permute-start | bytes 786440 | tf_op jit(solution)/shard_map/ppermute | solution.py:36
  162.0 13.7 %collective-permute-start.34 = (f32[8,2,32,128]{3,2,1,0:T(8,128)}, f32[8,2,32,128]{3,2,1,0:T(8,128)S(1)}, u32[]{:S(2)}, u32[]{:S(2)}) collective-permute-start(f32[8,2,32,128]{3,2,1,0:T(8,128)} %get-tuple-element.73), channel_id=1, source_target_pairs={{0,4},{2,6},{4,0},{6,2},{1,5},{3,7},{5,1},{7,3},{8,12},{10,14},{12... | collective-permute-start | bytes 786440 | tf_op jit(solution)/shard_map/ppermute | solution.py:36
  162.3 13.4 %collective-permute-start.33 = (f32[8,2,32,128]{3,2,1,0:T(8,128)}, f32[8,2,32,128]{3,2,1,0:T(8,128)S(1)}, u32[]{:S(2)}, u32[]{:S(2)}) collective-permute-start(f32[8,2,32,128]{3,2,1,0:T(8,128)} %get-tuple-element.72), channel_id=1, source_target_pairs={{0,1},{1,0},{2,3},{3,2},{4,5},{5,4},{6,7},{7,6},{8,9},{9,8},{10,11... | collective-permute-start | bytes 786440 | tf_op jit(solution)/shard_map/ppermute | solution.py:36
  176.7 8.3 %collective-permute-start.20 = (f32[8,2,32,128]{3,2,1,0:T(8,128)S(1)}, f32[8,2,32,128]{3,2,1,0:T(8,128)S(1)}, u32[]{:S(2)}, u32[]{:S(2)}) collective-permute-start(f32[8,2,32,128]{3,2,1,0:T(8,128)S(1)} %get-tuple-element.102), channel_id=1, source_target_pairs={{0,8},{8,0},{16,24},{24,16},{1,9},{9,1},{17,25},{25,17},{2,10},{10... | collective-permute-start | bytes 786440 | tf_op jit(solution)/shard_map/ppermute | solution.py:36
  185.1 25.2 %collective-permute-start.26 = (f32[16,2,32,128]{3,2,1,0:T(8,128)S(1)}, f32[16,2,32,128]{3,2,1,0:T(8,128)S(1)}, u32[]{:S(2)}, u32[]{:S(2)}) collective-permute-start(f32[16,2,32,128]{3,2,1,0:T(8,128)S(1)} %pad_maximum_fusion.1.refs_0_), channel_id=1, source_target_pairs={{0,16},{8,24},{16,0},{24,8},{1,17},{9,25},{17,1},{25,9},{2,18},{10... | collective-permute-start | bytes 1572872 | tf_op jit(solution)/shard_map/ppermute | solution.py:36
  187.5 25.0 %collective-permute-start.21 = (f32[16,2,32,128]{3,2,1,0:T(8,128)S(1)}, f32[16,2,32,128]{3,2,1,0:T(8,128)S(1)}, u32[]{:S(2)}, u32[]{:S(2)}) collective-permute-start(f32[16,2,32,128]{3,2,1,0:T(8,128)S(1)} %pad_maximum_fusion.1.refs_0_), channel_id=1, source_target_pairs={{0,1},{1,0},{2,3},{3,2},{4,5},{5,4},{6,7},{7,6},{8,9},{9,8},{10,11... | collective-permute-start | bytes 1572872 | tf_op jit(solution)/shard_map/ppermute | solution.py:36
  188.0 25.3 %collective-permute-start.22 = (f32[16,2,32,128]{3,2,1,0:T(8,128)S(1)}, f32[16,2,32,128]{3,2,1,0:T(8,128)S(1)}, u32[]{:S(2)}, u32[]{:S(2)}) collective-permute-start(f32[16,2,32,128]{3,2,1,0:T(8,128)S(1)} %pad_maximum_fusion.1.refs_0_), channel_id=1, source_target_pairs={{0,4},{2,6},{4,0},{6,2},{1,5},{3,7},{5,1},{7,3},{8,12},{10,14},{12... | collective-permute-start | bytes 1572872 | tf_op jit(solution)/shard_map/ppermute | solution.py:36
  210.3 14.8 %collective-permute-start.27 = (f32[16,2,32,128]{3,2,1,0:T(8,128)S(1)}, f32[16,2,32,128]{3,2,1,0:T(8,128)S(1)}, u32[]{:S(2)}, u32[]{:S(2)}) collective-permute-start(f32[16,2,32,128]{3,2,1,0:T(8,128)S(1)} %collective-permute-done.26.refs_0_), channel_id=1, source_target_pairs={{0,1},{1,0},{2,3},{3,2},{4,5},{5,4},{6,7},{7,6},{8,9},{9,8},{10,11... | collective-permute-start | bytes 1572872 | tf_op jit(solution)/shard_map/ppermute | solution.py:36
  210.6 14.8 %collective-permute-start.28 = (f32[16,2,32,128]{3,2,1,0:T(8,128)S(1)}, f32[16,2,32,128]{3,2,1,0:T(8,128)S(1)}, u32[]{:S(2)}, u32[]{:S(2)}) collective-permute-start(f32[16,2,32,128]{3,2,1,0:T(8,128)S(1)} %collective-permute-done.26.refs_0_), channel_id=1, source_target_pairs={{0,4},{2,6},{4,0},{6,2},{1,5},{3,7},{5,1},{7,3},{8,12},{10,14},{12... | collective-permute-start | bytes 1572872 | tf_op jit(solution)/shard_map/ppermute | solution.py:36
  212.5 18.5 %collective-permute-start.23 = (f32[8,2,32,128]{3,2,1,0:T(8,128)S(1)}, f32[8,2,32,128]{3,2,1,0:T(8,128)S(1)}, u32[]{:S(2)}, u32[]{:S(2)}) collective-permute-start(f32[8,2,32,128]{3,2,1,0:T(8,128)S(1)} %slice.108), channel_id=1, source_target_pairs={{0,4},{2,6},{4,0},{6,2},{1,5},{3,7},{5,1},{7,3},{8,12},{10,14},{12... | collective-permute-start | bytes 786440 | tf_op jit(solution)/shard_map/ppermute | solution.py:36
  213.3 18.4 %collective-permute-start.24 = (f32[8,2,32,128]{3,2,1,0:T(8,128)S(1)}, f32[8,2,32,128]{3,2,1,0:T(8,128)}, u32[]{:S(2)}, u32[]{:S(2)}) collective-permute-start(f32[8,2,32,128]{3,2,1,0:T(8,128)S(1)} %slice.109), channel_id=1, source_target_pairs={{0,1},{1,0},{2,3},{3,2},{4,5},{5,4},{6,7},{7,6},{8,9},{9,8},{10,11... | collective-permute-start | bytes 786440 | tf_op jit(solution)/shard_map/ppermute | solution.py:36
  225.1 14.8 %collective-permute-start.29 = (f32[8,2,32,128]{3,2,1,0:T(8,128)S(1)}, f32[8,2,32,128]{3,2,1,0:T(8,128)S(1)}, u32[]{:S(2)}, u32[]{:S(2)}) collective-permute-start(f32[8,2,32,128]{3,2,1,0:T(8,128)S(1)} %slice.110), channel_id=1, source_target_pairs={{0,4},{2,6},{4,0},{6,2},{1,5},{3,7},{5,1},{7,3},{8,12},{10,14},{12... | collective-permute-start | bytes 786440 | tf_op jit(solution)/shard_map/ppermute | solution.py:36
  225.4 14.5 %collective-permute-start.30 = (f32[8,2,32,128]{3,2,1,0:T(8,128)S(1)}, f32[8,2,32,128]{3,2,1,0:T(8,128)}, u32[]{:S(2)}, u32[]{:S(2)}) collective-permute-start(f32[8,2,32,128]{3,2,1,0:T(8,128)S(1)} %slice.111), channel_id=1, source_target_pairs={{0,1},{1,0},{2,3},{3,2},{4,5},{5,4},{6,7},{7,6},{8,9},{9,8},{10,11... | collective-permute-start | bytes 786440 | tf_op jit(solution)/shard_map/ppermute | solution.py:36
  239.9 9.4 %collective-permute-start.25 = (f32[16,2,64,128]{3,2,1,0:T(8,128)}, f32[16,2,64,128]{3,2,1,0:T(8,128)S(1)}, u32[]{:S(2)}, u32[]{:S(2)}) collective-permute-start(f32[16,2,64,128]{3,2,1,0:T(8,128)} %get-tuple-element.65), channel_id=1, source_target_pairs={{0,2},{2,0},{4,6},{6,4},{1,3},{3,1},{5,7},{7,5},{8,10},{10,8},{12,... | collective-permute-start | bytes 3145736 | tf_op jit(solution)/shard_map/ppermute | solution.py:36
  248.8 3.0 collective-permute-start.31
  266.6 2.2 collective-permute-start.48
  276.4 10.3 %collective-permute-start.51 = (f32[8,2,32,128]{3,2,1,0:T(8,128)}, f32[8,2,32,128]{3,2,1,0:T(8,128)S(1)}, u32[]{:S(2)}, u32[]{:S(2)}) collective-permute-start(f32[8,2,32,128]{3,2,1,0:T(8,128)} %get-tuple-element.84), channel_id=1, source_target_pairs={{0,5},{1,4},{2,7},{3,6},{4,1},{5,0},{6,3},{7,2},{8,13},{9,12},{10,... | collective-permute-start | bytes 786440 | tf_op jit(solution)/shard_map/ppermute | solution.py:36
  277.7 14.0 %collective-permute-start.50 = (f32[8,2,32,128]{3,2,1,0:T(8,128)}, f32[8,2,32,128]{3,2,1,0:T(8,128)S(1)}, u32[]{:S(2)}, u32[]{:S(2)}) collective-permute-start(f32[8,2,32,128]{3,2,1,0:T(8,128)} %get-tuple-element.83), channel_id=1, source_target_pairs={{0,4},{2,6},{4,0},{6,2},{1,5},{3,7},{5,1},{7,3},{8,12},{10,14},{12... | collective-permute-start | bytes 786440 | tf_op jit(solution)/shard_map/ppermute | solution.py:36
  279.6 12.6 %collective-permute-start.49 = (f32[8,2,32,128]{3,2,1,0:T(8,128)}, f32[8,2,32,128]{3,2,1,0:T(8,128)S(1)}, u32[]{:S(2)}, u32[]{:S(2)}) collective-permute-start(f32[8,2,32,128]{3,2,1,0:T(8,128)} %get-tuple-element.82), channel_id=1, source_target_pairs={{0,1},{1,0},{2,3},{3,2},{4,5},{5,4},{6,7},{7,6},{8,9},{9,8},{10,11... | collective-permute-start | bytes 786440 | tf_op jit(solution)/shard_map/ppermute | solution.py:36
  293.3 9.2 %collective-permute-start.36 = (f32[8,2,32,128]{3,2,1,0:T(8,128)S(1)}, f32[8,2,32,128]{3,2,1,0:T(8,128)S(1)}, u32[]{:S(2)}, u32[]{:S(2)}) collective-permute-start(f32[8,2,32,128]{3,2,1,0:T(8,128)S(1)} %get-tuple-element.100), channel_id=1, source_target_pairs={{0,8},{8,0},{16,24},{24,16},{1,9},{9,1},{17,25},{25,17},{2,10},{10... | collective-permute-start | bytes 786440 | tf_op jit(solution)/shard_map/ppermute | solution.py:36
  294.2 15.4 %collective-permute-start.52 = (f32[8,2,32,128]{3,2,1,0:T(8,128)S(1)}, f32[8,2,32,128]{3,2,1,0:T(8,128)S(1)}, u32[]{:S(2)}, u32[]{:S(2)}) collective-permute-start(f32[8,2,32,128]{3,2,1,0:T(8,128)S(1)} %pad_maximum_fusion.11), channel_id=1, source_target_pairs={{0,8},{8,0},{16,24},{24,16},{1,9},{9,1},{17,25},{25,17},{2,10},{10... | collective-permute-start | bytes 786440 | tf_op jit(solution)/shard_map/ppermute | solution.py:36
  302.6 14.8 %collective-permute-start.37 = (f32[16,2,32,128]{3,2,1,0:T(8,128)S(1)}, f32[16,2,32,128]{3,2,1,0:T(8,128)S(1)}, u32[]{:S(2)}, u32[]{:S(2)}) collective-permute-start(f32[16,2,32,128]{3,2,1,0:T(8,128)S(1)} %pad_maximum_fusion.2.refs_0_), channel_id=1, source_target_pairs={{0,1},{1,0},{2,3},{3,2},{4,5},{5,4},{6,7},{7,6},{8,9},{9,8},{10,11... | collective-permute-start | bytes 1572872 | tf_op jit(solution)/shard_map/ppermute | solution.py:36
  303.9 39.9 %collective-permute-start.38 = (f32[16,2,32,128]{3,2,1,0:T(8,128)S(1)}, f32[16,2,32,128]{3,2,1,0:T(8,128)S(1)}, u32[]{:S(2)}, u32[]{:S(2)}) collective-permute-start(f32[16,2,32,128]{3,2,1,0:T(8,128)S(1)} %pad_maximum_fusion.2.refs_0_), channel_id=1, source_target_pairs={{0,4},{2,6},{4,0},{6,2},{1,5},{3,7},{5,1},{7,3},{8,12},{10,14},{12... | collective-permute-start | bytes 1572872 | tf_op jit(solution)/shard_map/ppermute | solution.py:36
  304.5 37.4 %collective-permute-start.42 = (f32[16,2,32,128]{3,2,1,0:T(8,128)S(1)}, f32[16,2,32,128]{3,2,1,0:T(8,128)S(1)}, u32[]{:S(2)}, u32[]{:S(2)}) collective-permute-start(f32[16,2,32,128]{3,2,1,0:T(8,128)S(1)} %pad_maximum_fusion.2.refs_0_), channel_id=1, source_target_pairs={{0,16},{8,24},{16,0},{24,8},{1,17},{9,25},{17,1},{25,9},{2,18},{10... | collective-permute-start | bytes 1572872 | tf_op jit(solution)/shard_map/ppermute | solution.py:36
  309.6 34.4 %collective-permute-start.53 = (f32[16,2,32,128]{3,2,1,0:T(8,128)S(1)}, f32[16,2,32,128]{3,2,1,0:T(8,128)S(1)}, u32[]{:S(2)}, u32[]{:S(2)}) collective-permute-start(f32[16,2,32,128]{3,2,1,0:T(8,128)S(1)} %pad_maximum_fusion.3.refs_0_), channel_id=1, source_target_pairs={{0,1},{1,0},{2,3},{3,2},{4,5},{5,4},{6,7},{7,6},{8,9},{9,8},{10,11... | collective-permute-start | bytes 1572872 | tf_op jit(solution)/shard_map/ppermute | solution.py:36
  311.6 39.1 %collective-permute-start.58 = (f32[16,2,32,128]{3,2,1,0:T(8,128)S(1)}, f32[16,2,32,128]{3,2,1,0:T(8,128)}, u32[]{:S(2)}, u32[]{:S(2)}) collective-permute-start(f32[16,2,32,128]{3,2,1,0:T(8,128)S(1)} %pad_maximum_fusion.3.refs_0_), channel_id=1, source_target_pairs={{0,16},{8,24},{16,0},{24,8},{1,17},{9,25},{17,1},{25,9},{2,18},{10... | collective-permute-start | bytes 1572872 | tf_op jit(solution)/shard_map/ppermute | solution.py:36
  317.4 35.0 %collective-permute-start.54 = (f32[16,2,32,128]{3,2,1,0:T(8,128)S(1)}, f32[16,2,32,128]{3,2,1,0:T(8,128)S(1)}, u32[]{:S(2)}, u32[]{:S(2)}) collective-permute-start(f32[16,2,32,128]{3,2,1,0:T(8,128)S(1)} %pad_maximum_fusion.3.refs_0_), channel_id=1, source_target_pairs={{0,4},{2,6},{4,0},{6,2},{1,5},{3,7},{5,1},{7,3},{8,12},{10,14},{12... | collective-permute-start | bytes 1572872 | tf_op jit(solution)/shard_map/ppermute | solution.py:36
  341.9 21.6 %collective-permute-start.43 = (f32[16,2,32,128]{3,2,1,0:T(8,128)S(1)}, f32[16,2,32,128]{3,2,1,0:T(8,128)S(1)}, u32[]{:S(2)}, u32[]{:S(2)}) collective-permute-start(f32[16,2,32,128]{3,2,1,0:T(8,128)S(1)} %collective-permute-done.42.refs_0_), channel_id=1, source_target_pairs={{0,1},{1,0},{2,3},{3,2},{4,5},{5,4},{6,7},{7,6},{8,9},{9,8},{10,11... | collective-permute-start | bytes 1572872 | tf_op jit(solution)/shard_map/ppermute | solution.py:36
  343.7 20.9 %collective-permute-start.44 = (f32[16,2,32,128]{3,2,1,0:T(8,128)S(1)}, f32[16,2,32,128]{3,2,1,0:T(8,128)S(1)}, u32[]{:S(2)}, u32[]{:S(2)}) collective-permute-start(f32[16,2,32,128]{3,2,1,0:T(8,128)S(1)} %collective-permute-done.42.refs_0_), channel_id=1, source_target_pairs={{0,4},{2,6},{4,0},{6,2},{1,5},{3,7},{5,1},{7,3},{8,12},{10,14},{12... | collective-permute-start | bytes 1572872 | tf_op jit(solution)/shard_map/ppermute | solution.py:36
  344.0 18.9 %collective-permute-start.39 = (f32[8,2,32,128]{3,2,1,0:T(8,128)S(1)}, f32[8,2,32,128]{3,2,1,0:T(8,128)S(1)}, u32[]{:S(2)}, u32[]{:S(2)}) collective-permute-start(f32[8,2,32,128]{3,2,1,0:T(8,128)S(1)} %slice.114), channel_id=1, source_target_pairs={{0,4},{2,6},{4,0},{6,2},{1,5},{3,7},{5,1},{7,3},{8,12},{10,14},{12... | collective-permute-start | bytes 786440 | tf_op jit(solution)/shard_map/ppermute | solution.py:36
  350.7 22.1 %collective-permute-start.59 = (f32[16,2,32,128]{3,2,1,0:T(8,128)}, f32[16,2,32,128]{3,2,1,0:T(8,128)S(1)}, u32[]{:S(2)}, u32[]{:S(2)}) collective-permute-start(f32[16,2,32,128]{3,2,1,0:T(8,128)} %collective-permute-done.58.refs_0_), channel_id=1, source_target_pairs={{0,1},{1,0},{2,3},{3,2},{4,5},{5,4},{6,7},{7,6},{8,9},{9,8},{10,11... | collective-permute-start | bytes 1572872 | tf_op jit(solution)/shard_map/ppermute | solution.py:36
  352.3 29.7 %collective-permute-start.60 = (f32[16,2,32,128]{3,2,1,0:T(8,128)}, f32[16,2,32,128]{3,2,1,0:T(8,128)}, u32[]{:S(2)}, u32[]{:S(2)}) collective-permute-start(f32[16,2,32,128]{3,2,1,0:T(8,128)} %collective-permute-done.58.refs_0_), channel_id=1, source_target_pairs={{0,4},{2,6},{4,0},{6,2},{1,5},{3,7},{5,1},{7,3},{8,12},{10,14},{12... | collective-permute-start | bytes 1572872 | tf_op jit(solution)/shard_map/ppermute | solution.py:36
  362.8 9.2 %collective-permute-start.40 = (f32[8,2,32,128]{3,2,1,0:T(8,128)S(1)}, f32[8,2,32,128]{3,2,1,0:T(8,128)S(1)}, u32[]{:S(2)}, u32[]{:S(2)}) collective-permute-start(f32[8,2,32,128]{3,2,1,0:T(8,128)S(1)} %slice.115), channel_id=1, source_target_pairs={{0,1},{1,0},{2,3},{3,2},{4,5},{5,4},{6,7},{7,6},{8,9},{9,8},{10,11... | collective-permute-start | bytes 786440 | tf_op jit(solution)/shard_map/ppermute | solution.py:36
  363.5 20.3 %collective-permute-start.55 = (f32[8,2,32,128]{3,2,1,0:T(8,128)S(1)}, f32[8,2,32,128]{3,2,1,0:T(8,128)}, u32[]{:S(2)}, u32[]{:S(2)}) collective-permute-start(f32[8,2,32,128]{3,2,1,0:T(8,128)S(1)} %slice.120), channel_id=1, source_target_pairs={{0,4},{2,6},{4,0},{6,2},{1,5},{3,7},{5,1},{7,3},{8,12},{10,14},{12... | collective-permute-start | bytes 786440 | tf_op jit(solution)/shard_map/ppermute | solution.py:36
  364.7 20.4 %collective-permute-start.56 = (f32[8,2,32,128]{3,2,1,0:T(8,128)S(1)}, f32[8,2,32,128]{3,2,1,0:T(8,128)}, u32[]{:S(2)}, u32[]{:S(2)}) collective-permute-start(f32[8,2,32,128]{3,2,1,0:T(8,128)S(1)} %slice.121), channel_id=1, source_target_pairs={{0,1},{1,0},{2,3},{3,2},{4,5},{5,4},{6,7},{7,6},{8,9},{9,8},{10,11... | collective-permute-start | bytes 786440 | tf_op jit(solution)/shard_map/ppermute | solution.py:36
  372.0 22.4 %collective-permute-start.45 = (f32[8,2,32,128]{3,2,1,0:T(8,128)S(1)}, f32[8,2,32,128]{3,2,1,0:T(8,128)}, u32[]{:S(2)}, u32[]{:S(2)}) collective-permute-start(f32[8,2,32,128]{3,2,1,0:T(8,128)S(1)} %slice.116), channel_id=1, source_target_pairs={{0,4},{2,6},{4,0},{6,2},{1,5},{3,7},{5,1},{7,3},{8,12},{10,14},{12... | collective-permute-start | bytes 786440 | tf_op jit(solution)/shard_map/ppermute | solution.py:36
  372.8 21.7 %collective-permute-start.46 = (f32[8,2,32,128]{3,2,1,0:T(8,128)S(1)}, f32[8,2,32,128]{3,2,1,0:T(8,128)}, u32[]{:S(2)}, u32[]{:S(2)}) collective-permute-start(f32[8,2,32,128]{3,2,1,0:T(8,128)S(1)} %slice.117), channel_id=1, source_target_pairs={{0,1},{1,0},{2,3},{3,2},{4,5},{5,4},{6,7},{7,6},{8,9},{9,8},{10,11... | collective-permute-start | bytes 786440 | tf_op jit(solution)/shard_map/ppermute | solution.py:36
  382.1 30.1 %collective-permute-start.41 = (f32[16,2,64,128]{3,2,1,0:T(8,128)}, f32[16,2,64,128]{3,2,1,0:T(8,128)S(1)}, u32[]{:S(2)}, u32[]{:S(2)}) collective-permute-start(f32[16,2,64,128]{3,2,1,0:T(8,128)} %get-tuple-element.76), channel_id=1, source_target_pairs={{0,2},{2,0},{4,6},{6,4},{1,3},{3,1},{5,7},{7,5},{8,10},{10,8},{12,... | collective-permute-start | bytes 3145736 | tf_op jit(solution)/shard_map/ppermute | solution.py:36
  383.8 19.4 %collective-permute-start.61 = (f32[8,2,32,128]{3,2,1,0:T(8,128)S(1)}, f32[8,2,32,128]{3,2,1,0:T(8,128)}, u32[]{:S(2)}, u32[]{:S(2)}) collective-permute-start(f32[8,2,32,128]{3,2,1,0:T(8,128)S(1)} %slice.122), channel_id=1, source_target_pairs={{0,4},{2,6},{4,0},{6,2},{1,5},{3,7},{5,1},{7,3},{8,12},{10,14},{12... | collective-permute-start | bytes 786440 | tf_op jit(solution)/shard_map/ppermute | solution.py:36
  385.1 18.2 %collective-permute-start.62 = (f32[8,2,32,128]{3,2,1,0:T(8,128)}, f32[8,2,32,128]{3,2,1,0:T(8,128)}, u32[]{:S(2)}, u32[]{:S(2)}) collective-permute-start(f32[8,2,32,128]{3,2,1,0:T(8,128)} %slice.123), channel_id=1, source_target_pairs={{0,1},{1,0},{2,3},{3,2},{4,5},{5,4},{6,7},{7,6},{8,9},{9,8},{10,11... | collective-permute-start | bytes 786440 | tf_op jit(solution)/shard_map/ppermute | solution.py:36
  394.4 36.2 %collective-permute-start.57 = (f32[16,2,64,128]{3,2,1,0:T(8,128)}, f32[16,2,64,128]{3,2,1,0:T(8,128)S(1)}, u32[]{:S(2)}, u32[]{:S(2)}) collective-permute-start(f32[16,2,64,128]{3,2,1,0:T(8,128)} %get-tuple-element.86), channel_id=1, source_target_pairs={{0,2},{2,0},{4,6},{6,4},{1,3},{3,1},{5,7},{7,5},{8,10},{10,8},{12,... | collective-permute-start | bytes 3145736 | tf_op jit(solution)/shard_map/ppermute | solution.py:36
  402.8 9.4 %collective-permute-start.47 = (f32[16,2,64,128]{3,2,1,0:T(8,128)}, f32[16,2,64,128]{3,2,1,0:T(8,128)S(1)}, u32[]{:S(2)}, u32[]{:S(2)}) collective-permute-start(f32[16,2,64,128]{3,2,1,0:T(8,128)} %get-tuple-element.78), channel_id=1, source_target_pairs={{0,2},{2,0},{4,6},{6,4},{1,3},{3,1},{5,7},{7,5},{8,10},{10,8},{12,... | collective-permute-start | bytes 3145736 | tf_op jit(solution)/shard_map/ppermute | solution.py:36
  411.5 19.1 %collective-permute-start.63 = (f32[16,2,64,128]{3,2,1,0:T(8,128)}, f32[16,2,64,128]{3,2,1,0:T(8,128)}, u32[]{:S(2)}, u32[]{:S(2)}) collective-permute-start(f32[16,2,64,128]{3,2,1,0:T(8,128)} %get-tuple-element.88), channel_id=1, source_target_pairs={{0,2},{2,0},{4,6},{6,4},{1,3},{3,1},{5,7},{7,5},{8,10},{10,8},{12,... | collective-permute-start | bytes 3145736 | tf_op jit(solution)/shard_map/ppermute | solution.py:36
  (37 other events, 561.0 us)
